TPU v7x, 256 devices: a whole 4x4x8 slice. The times are simulated.
256 devices in a mesh: dp: 16 (over x_lo, y, core), tensor: 16 (over z, x_hi).
Axes of the slice: x: 4 (x_hi: 2, x_lo: 2; x = x_hi * 2 + x_lo), y: 4, z: 8, core: 2. Of those that a mesh axis runs over, the one named last changes fastest.
Arguments:
- target_hidden: bfloat16 [512, 16384], P('dp', 'tensor'), may hold values from -64 to 64
- target_gain: bfloat16 [16384], replicated, may hold values from 0.25 to 1.75
- target_head: bfloat16 [16384, 65536], P(None, ('dp', 'tensor')), may hold values from -8 to 8
- reference_hidden: bfloat16 [512, 4096], P('dp', 'tensor'), may hold values from -64 to 64
- reference_gain: bfloat16 [4096], replicated, may hold values from 0.25 to 1.75
- reference_head: bfloat16 [4096, 65536], P(None, ('dp', 'tensor')), may hold values from -8 to 8
Outputs:
- contrast: float32 [512, 65536], P(None, ('dp', 'tensor'))
All inputs are finite; a program needn't handle non-finite values.
Results may differ from a plain program's by a relative error of at most 0.0012.
Values may be sent and summed in bfloat16 or wider, within the bound.
No kernel may reach another device: no remote copies, remote signals or barrier semaphores. Data moves between devices by JAX's collectives and lax.ppermute only.
A program may use at most 128 MiB of HBM per device.

v0:
```python
import jax
import jax.numpy as jnp
from jax import lax
from jax.sharding import PartitionSpec as P

EPS = 1e-05
LOG_TEN = 2.302585092994046


def normalize_full(piece, gain):
    values = piece.astype(jnp.float32)
    square_mean = jnp.mean(values * values, axis=1, keepdims=True)
    return (values * lax.rsqrt(square_mean + EPS) * gain.astype(jnp.float32)).astype(jnp.bfloat16)


def local(
    target_hidden, target_gain, target_head, reference_hidden, reference_gain, reference_head
):
    wide_t, wide_r = (
        lax.all_gather(target_hidden, "tensor", axis=1, tiled=True),
        lax.all_gather(reference_hidden, "tensor", axis=1, tiled=True),
    )
    logits_t = jnp.dot(
        normalize_full(lax.all_gather(wide_t, "dp", axis=0, tiled=True), target_gain),
        target_head,
        preferred_element_type=jnp.float32,
    )
    logits_r = jnp.dot(
        normalize_full(lax.all_gather(wide_r, "dp", axis=0, tiled=True), reference_gain),
        reference_head,
        preferred_element_type=jnp.float32,
    )
    local_peak_t = jnp.max(logits_t, axis=1)
    local_peak_r = jnp.max(logits_r, axis=1)
    peak_t, peak_r = lax.pmax((local_peak_t, local_peak_r), ("dp", "tensor"))
    local_total_t = jnp.sum(jnp.exp(logits_t - peak_t[:, None]), axis=1)
    local_total_r = jnp.sum(jnp.exp(logits_r - peak_r[:, None]), axis=1)
    total_t, total_r = lax.psum((local_total_t, local_total_r), ("dp", "tensor"))
    lse_t = (peak_t + jnp.log(total_t))[:, None]
    lse_r = (peak_r + jnp.log(total_r))[:, None]
    margin = jnp.minimum(0.0, logits_t - peak_t[:, None] + LOG_TEN)
    return logits_t - lse_t - 0.5 * (logits_r - lse_r) + margin


def solution(mesh):
    placed = (
        P("dp", "tensor"),
        P(),
        P(None, ("dp", "tensor")),
        P("dp", "tensor"),
        P(),
        P(None, ("dp", "tensor")),
    )
    return jax.shard_map(
        local, mesh=mesh, in_specs=placed, out_specs=P(None, ("dp", "tensor")), check_vma=False
    )
```

profile of v0, /device:TPU:1, one launch (start us, length us, event | category | flops | bytes accessed | tf_op | source)
XLA Modules:
  0.0 408.6 jit_solution(10341636960921009847)
XLA Ops:
  6.5 0.0 copy-start
  6.5 0.0 all-gather.4.cloned.1.call-start
  6.5 0.7 all-gather.4.cloned.1.call-update
  7.3 0.0 all-gather.8.cloned.1.call-start
  7.3 42.1 %all_gather.14 = bf16[32,4096]{1,0:T(8,128)(2,1)} all-gather(bf16[32,256]{1,0:T(8,128)(2,1)} %param.9), channel_id=1, replica_groups=mesh['dp'=16,'tensor'=16] {'tensor'}, dimensions={1}, use_global_device_ids=true | all-gather | bytes 278528 | tf_op jit(solution)/shard_map/all_gather | solution.py:21
  49.4 0.0 all-gather.8.cloned.1.call-update
  49.5 0.0 all-gather.6.cloned.1.call-start
  49.5 39.4 %all-gather.4.cloned.1.call-done = bf16[32,16384]{1,0:T(8,128)(2,1)} async-done(((bf16[32,1024]{1,0:T(8,128)(2,1)}), bf16[32,16384]{1,0:T(8,128)(2,1)}) %all-gather.4.cloned.1.call-update) | async-done | bytes 1048592 | tf_op jit(solution)/shard_map/all_gather | solution.py:20
  88.9 0.0 all-gather.6.cloned.1.call-update
  88.9 0.7 convert_element_type.22
  89.6 0.8 convert_element_type.19
  90.4 41.0 %all-gather.8.cloned.1.call-done = bf16[512,4096]{1,0:T(8,128)(2,1)} async-done(((bf16[32,4096]{1,0:T(8,128)(2,1)}), bf16[512,4096]{1,0:T(8,128)(2,1)}) %all-gather.8.cloned.1.call-update) | async-done | bytes 4194320 | tf_op jit(solution)/shard_map/all_gather | solution.py:29
  131.4 3.1 fusion.7
  134.5 0.0 copy-done
  134.5 3.8 fusion.14
  138.3 89.3 %all-gather.6.cloned.1.call-done = bf16[512,16384]{1,0:T(8,128)(2,1)} async-done(((bf16[32,16384]{1,0:T(8,128)(2,1)}), bf16[512,16384]{1,0:T(8,128)(2,1)}) %all-gather.6.cloned.1.call-update) | async-done | bytes 16777232 | tf_op jit(solution)/shard_map/all_gather | solution.py:24
  227.5 7.2 %fusion = f32[512]{0:T(512)S(1)} fusion(bf16[512,16384]{1,0:T(8,128)(2,1)} %all-gather.6.cloned.1.call-done), kind=kLoop, calls=%fused_computation.2 | loop fusion | flops 25165312 | bytes 16779264 | tf_op jit(solution)/shard_map/reduce_sum | solution.py:12
  234.7 13.6 %fusion.15 = (f32[512]{0:T(512)S(1)}, f32[512,256]{0,1:T(8,128)S(1)}) fusion(bf16[16384,256]{1,0:T(8,128)(2,1)} %param.8, bf16[512,16384]{1,0:T(8,128)(2,1)} %all-gather.6.cloned.1.call-done, f32[16384]{0:T(1024)S(1)} %convert_element_type.19, f32[512]{0:T(512)S(1)} %add_rsqrt_fusion.1), kind=kOutput, calls=%fused_computation.24 | convolution fusion | flops 4328652288 | bytes 25759744 | tf_op jit(solution)/shard_map/dot_general | solution.py:23
  248.4 77.0 %all-reduce.1 = (f32[512]{0:T(512)S(1)}, f32[512]{0:T(512)S(1)}) all-reduce(f32[512]{0:T(512)S(1)} %get-tuple-element.9, f32[512]{0:T(512)S(1)} %get-tuple-element.11), channel_id=1, replica_groups=mesh['dp'=16,'tensor'=16] {'dp','tensor'}, use_global_device_ids=true, to_apply=%region_7.0 | all-reduce | flops 1024 | bytes 8192 | tf_op jit(solution)/shard_map/pmax | solution.py:35
  325.4 0.2 exponential_reduce_fusion
  325.6 73.6 %all-reduce = (f32[512]{0:T(512)S(1)}, f32[512]{0:T(512)S(1)}) all-reduce(f32[512]{0:T(512)S(1)} %get-tuple-element.13, f32[512]{0:T(512)S(1)} %get-tuple-element.14), channel_id=1, replica_groups=mesh['dp'=16,'tensor'=16] {'dp','tensor'}, use_global_device_ids=true, to_apply=%region_9.0 | all-reduce | flops 1024 | bytes 8192 | tf_op jit(solution)/shard_map/psum | solution.py:38
  399.1 0.9 minimum_add_fusion
  400.1 2.0 copy.7
  (4 shorter events, 0.0 us)
Async XLA Ops:
  6.5 128.0 %copy-start = (bf16[4096,256]{1,0:T(8,128)(2,1)S(1)}, bf16[4096,256]{1,0:T(8,128)(2,1)}, u32[]{:S(2)}) copy-start(bf16[4096,256]{1,0:T(8,128)(2,1)} %param.11) | copy-start | bytes 6291460
  6.5 82.4 %all-gather.4.cloned.1.call-start = ((), (), s32[]{:S(2)}) async-start(), calls=%async_computation | async-start | bytes 1114112 | tf_op jit(solution)/shard_map/all_gather | solution.py:20
  7.3 124.1 %all-gather.8.cloned.1.call-start = ((), (), s32[]{:S(2)}) async-start(), calls=%async_computation.2 | async-start | bytes 4456448 | tf_op jit(solution)/shard_map/all_gather | solution.py:29
  49.5 178.1 %all-gather.6.cloned.1.call-start = ((), (), s32[]{:S(2)}) async-start(), calls=%async_computation.1 | async-start | bytes 17825792 | tf_op jit(solution)/shard_map/all_gather | solution.py:24
Sparse Core Ops, SparseCore 0:
  10.0 78.8 all-gather.3
  90.7 40.6 all-gather.7
  133.3 94.2 all-gather.5
where the time goes:
time: 409 us
  blocking collectives  193 us (47%)
  waiting for transfers between devices  170 us (42%)
  matrix products  17.4 us (4%)
  between operations  13.1 us (3%)
  other arithmetic  12.9 us (3%)
    all_gather x1, waiting for transfers between devices, local(): lax.all_gather(wide_t, 'dp', axis=0, tiled=True)  89.3 us
    pmax x1, blocking collectives, local(): peak_t, peak_r = lax.pmax((local_peak_t, local_peak_r), ('dp', 'tensor'))  77 us
    psum x1, blocking collectives, local(): lax.psum((local_total_t, local_total_r), ('dp', 'tensor'))  73.6 us
    all_gather x1, blocking collectives, local(): lax.all_gather(reference_hidden, 'tensor', axis=1, tiled=True)  42.1 us
    all_gather x1, waiting for transfers between devices, local(): lax.all_gather(wide_r, 'dp', axis=0, tiled=True)  41 us
    all_gather x1, waiting for transfers between devices, local(): lax.all_gather(target_hidden, 'tensor', axis=1, tiled=True)  39.4 us
    dot_general x1, matrix products, local(): jnp.dot(normalize_full(lax.all_gather(wide_t, 'dp', axis=0, tiled=True),...  13.6 us
    reduce_sum x2, other arithmetic, normalize_full(): square_mean = jnp.mean(values * values, axis=1, keepdims=True)  10.3 us
  transfers between devices with their start and end apart: 3, of which 3 were waited for; matrix products, arithmetic and copies ran while one was open for 2% of the time, Pallas kernels for 0%

commit v1 on v0

v1 whole, which is shorter than its diff:
```python
import functools

import jax
import jax.numpy as jnp
import numpy as np
from jax import lax
from jax.experimental import pallas as pl
from jax.experimental.pallas import tpu as pltpu
from jax.sharding import Mesh
from jax.sharding import PartitionSpec as P

EPS = 1e-05
LOG_TEN = 2.302585092994046

AXES = ("xl", "y", "core", "z", "xh")
SIZES = (2, 4, 2, 8, 2)
NX, NY, NZ = 4, 4, 8

D, DR = 16384, 4096
ROWS = 256
COLS = 256
GROUP = 32
WT, WR = 1024, 256
FA = 896
FC = WT - FA + WR
RING8 = (0, -1, 1, -2, 2, -3, 3, 4)


def flat_index(x, y, z, c):
    xl, xh = x % 2, x // 2
    return (((xl * NY + y) * 2 + c) * NZ + z) * 2 + xh


def send(value, move):
    pairs = []
    for xl, y, c, z, xh in np.ndindex(*SIZES):
        x = 2 * xh + xl
        tx, ty, tz, tc = move(x, y, z, c)
        pairs.append((flat_index(x, y, z, c), flat_index(tx % NX, ty % NY, tz % NZ, tc % 2)))
    return lax.ppermute(value, AXES, pairs)


PAIRS4 = ((1, 0, 3, 2), (3, 2, 1, 0))
PAIRS8 = ((1, 0, 3, 2, 5, 4, 7, 6), (7, 2, 1, 4, 3, 6, 5, 0), (3, 6, 5, 0, 7, 2, 1, 4))


def sources(pairs):
    rows = [[place] for place in range(len(pairs[0]))]
    for partner in pairs:
        rows = [rows[place] + rows[partner[place]] for place in range(len(rows))]
    return np.array(rows, np.int32)


def along_z(step):
    return lambda x, y, z, c: (x, y, z + step, c)


def pair_z(partner):
    return lambda x, y, z, c: (x, y, partner[z], c)


def pair_x(partner):
    return lambda x, y, z, c: (partner[x], y, z, c)


def pair_y(partner):
    return lambda x, y, z, c: (x, partner[y], z, c)


def pair_x_or_y(partner, x_core):
    return lambda x, y, z, c: (partner[x], y, z, c) if c == x_core else (x, partner[y], z, c)


def other_core(x, y, z, c):
    return (x, y, z, 1 - c)


def x_or_y(step, x_core):
    return lambda x, y, z, c: (x + step, y, z, c) if c == x_core else (x, y + step, z, c)


def after(value, *others):
    return lax.optimization_barrier((value,) + others)[0]


def ring8(value, core):
    low1 = send(value, along_z(1))
    high1 = send(value, along_z(-1))
    low2 = send(low1, along_z(1))
    high2 = send(high1, along_z(-1))
    low3 = send(low2, along_z(1))
    high3 = send(high2, along_z(-1))
    far = send(jnp.where(core == 0, low3, high3), lambda x, y, z, c: (x, y, z + 1 - 2 * c, c))
    return [value, low1, high1, low2, high2, low3, high3, far]


A_SLOTS = ((0, 0, 2), (0, 2, 2), (1, 0, 2), (1, 2, 2), (2, 0, 2), (2, 2, 2), (3, 0, 2), (3, 2, 2))
NA = len(A_SLOTS)
AHEAD = 2


def heads_kernel(*refs):
    table_ref, gain_t_ref, gain_r_ref = refs[:3]
    a_refs, c_refs, head_refs = refs[3 : 3 + NA], refs[3 + NA : 11 + NA], refs[11 + NA : 15 + NA]
    head_t_own, head_t_other, head_r_own, head_r_other = head_refs
    logits_own, logits_cross, stats_ref = refs[15 + NA : 18 + NA]
    buf_a, buf_c, buf_t, buf_r = refs[18 + NA : 22 + NA]
    scale_t, scale_r, sums, left_t0, left_r0, left_t1, left_r1, sum_t, sum_r, sem_x, sem_h = refs[22 + NA :]
    lefts = ((left_t0, left_r0), (left_t1, left_r1))

    def hidden_copies(i, c_ref):
        out = []
        place_a = table_ref[72 + i]
        for n, (ref, (k, j, count)) in enumerate(zip(a_refs, A_SLOTS)):
            target = buf_a.at[i, k, pl.ds(j, count)]
            out.append(pltpu.make_async_copy(ref.at[:, place_a], target, sem_x.at[i, n]))
        out.append(pltpu.make_async_copy(c_ref, buf_c.at[i], sem_x.at[i, NA]))
        return out

    def head_copies(i):
        z = table_ref[32 + i]
        own, other = pl.ds(0, COLS), pl.ds(COLS, COLS)
        return [
            pltpu.make_async_copy(head_t_own.at[z], buf_t.at[i, :, own], sem_h.at[i, 0]),
            pltpu.make_async_copy(head_t_other.at[z], buf_t.at[i, :, other], sem_h.at[i, 1]),
            pltpu.make_async_copy(head_r_own.at[z], buf_r.at[i, :, own], sem_h.at[i, 2]),
            pltpu.make_async_copy(head_r_other.at[z], buf_r.at[i, :, other], sem_h.at[i, 3]),
        ]

    for i in range(NZ):
        for copy in hidden_copies(i, c_refs[i]):
            copy.start()
    def start_heads(i):
        for copy in head_copies(i):
            copy.start()

    for i in range(AHEAD):
        start_heads(i)

    sums[...] = jnp.zeros_like(sums)

    def square_step(i, carry):
        for copy in hidden_copies(i, c_refs[0]):
            copy.wait()

        def lanes(ref, low, high):
            total = None
            for at in range(low, high, 128):
                part = ref[:, at : at + 128].astype(jnp.float32)
                total = part * part if total is None else total + part * part
            return total

        for n in range(16):
            sums[0, n] += lanes(buf_a.at[i, n // 4, n % 4], 0, FA)
            sums[1, n] += lanes(buf_c.at[i, n], 0, WT - FA)
            sums[2, n] += lanes(buf_c.at[i, n], WT - FA, FC)
        return carry

    lax.fori_loop(0, NZ, square_step, 0)
    scale_t[...] = jnp.zeros_like(scale_t)
    scale_r[...] = jnp.zeros_like(scale_r)
    for n in range(16):
        scale_t[table_ref[n]] += sums[0, n]
        scale_t[table_ref[40 + n]] += sums[1, n]
        scale_r[table_ref[40 + n]] += sums[2, n]
    for scale, width in ((scale_t, D), (scale_r, DR)):
        mean = jnp.sum(scale[...], axis=2, keepdims=True) * (1.0 / width)
        scale[...] = jnp.broadcast_to(lax.rsqrt(mean + EPS), scale.shape)

    def place(i, left):
        left_t, left_r = left
        z = table_ref[32 + i]

        def put(source, at, scale, group, gain, target, xh, column, width):
            rows = pl.ds(pl.multiple_of(group * GROUP, GROUP), GROUP)
            value = source[:, at : at + 128].astype(jnp.float32)
            value = value * scale[group] * gain[z * 2 + xh][:, column : column + 128]
            to = pl.ds(pl.multiple_of(xh * width + column, 128), 128)
            target[rows, to] = value.astype(jnp.bfloat16)

        for n in range(16):
            group, xh = table_ref[n], table_ref[16 + n]
            for at in range(0, FA, 128):
                put(buf_a.at[i, n // 4, n % 4], at, scale_t, group, gain_t_ref, left_t, xh, at, WT)
            group, xh = table_ref[40 + n], table_ref[56 + n]
            for at in range(0, WT - FA, 128):
                put(buf_c.at[i, n], at, scale_t, group, gain_t_ref, left_t, xh, FA + at, WT)
            for at in range(0, WR, 128):
                source = buf_c.at[i, n]
                put(source, WT - FA + at, scale_r, group, gain_r_ref, left_r, xh, at, WR)

    sum_t[...] = jnp.zeros_like(sum_t)
    sum_r[...] = jnp.zeros_like(sum_r)

    def multiply(i, left):
        left_t, left_r = left
        sum_t[...] += jnp.dot(left_t[...], buf_t[i], preferred_element_type=jnp.float32)
        sum_r[...] += jnp.dot(left_r[...], buf_r[i], preferred_element_type=jnp.float32)

    def wait_heads(i):
        for copy in head_copies(i):
            copy.wait()

    place(0, lefts[0])

    def pair_step(pair, carry):
        i = pair * 2
        wait_heads(i)

        @pl.when(i + AHEAD < NZ)
        def _():
            start_heads(i + AHEAD)

        place(i + 1, lefts[1])
        multiply(i, lefts[0])
        wait_heads(i + 1)

        @pl.when(i + 1 + AHEAD < NZ)
        def _():
            start_heads(i + 1 + AHEAD)

        place(jnp.minimum(i + 2, NZ - 1), lefts[0])
        multiply(i + 1, lefts[1])
        return carry

    lax.fori_loop(0, NZ // 2, pair_step, 0)
    for model, total in enumerate((sum_t, sum_r)):
        logits_own[model] = total[:, :COLS]
        logits_cross[model] = total[:, COLS:]

    columns = []
    for model in range(2):
        one, two = logits_own[model], logits_cross[model]
        peak = jnp.max(jnp.maximum(one, two), axis=1, keepdims=True)
        total = jnp.sum(jnp.exp(one - peak) + jnp.exp(two - peak), axis=1, keepdims=True)
        columns.append((peak, total))
    lane = lax.broadcasted_iota(jnp.int32, (ROWS, 128), 1)
    packed = jnp.where(
        lane == 0,
        columns[0][0],
        jnp.where(lane == 1, columns[1][0], jnp.where(lane == 2, columns[0][1], columns[1][1])),
    )
    stats_ref[...] = packed.T[:8, :]


def contrast_kernel(core_ref, own_ref, other_ref, logits_own, logits_other, out_ref):
    core = core_ref[0]

    def score(stats, logits, where):
        logits_t, logits_r = logits[0], logits[1]
        tall = jnp.concatenate([stats, jnp.zeros((120, ROWS), jnp.float32)], axis=0).T
        peak_t, peak_r = tall[:, 0:1], tall[:, 1:2]
        lse_t = peak_t + jnp.log(tall[:, 2:3])
        lse_r = peak_r + jnp.log(tall[:, 3:4])
        margin = jnp.minimum(0.0, logits_t - peak_t + LOG_TEN)
        value = logits_t - lse_t - 0.5 * (logits_r - lse_r) + margin
        for group in range(ROWS // GROUP):
            out_ref[group, where] = value[group * GROUP : (group + 1) * GROUP]

    score(own_ref[...], logits_own, core)
    score(other_ref[...], logits_other, 1 - core)


def merge(parts):
    peaks = functools.reduce(jnp.maximum, [p[0:2] for p in parts])
    totals = sum(p[2:4] * jnp.exp(p[0:2] - peaks) for p in parts)
    return jnp.concatenate([peaks, totals, jnp.zeros_like(p8(parts[0]))], axis=0)


def p8(part):
    return part[4:8]


vmem = pl.BlockSpec(memory_space=pltpu.VMEM)
smem = pl.BlockSpec(memory_space=pltpu.SMEM)
hbm = pl.BlockSpec(memory_space=pl.ANY)


def heads_call(*operands):
    square = jax.ShapeDtypeStruct((2, ROWS, COLS), jnp.float32)
    bf16 = jnp.bfloat16
    return pl.pallas_call(
        heads_kernel,
        out_shape=[square] * 2 + [jax.ShapeDtypeStruct((8, ROWS), jnp.float32)],
        in_specs=[smem] + [vmem] * 2 + [hbm] * (NA + 12),
        out_specs=[vmem] * 3,
        scratch_shapes=[
            pltpu.VMEM((NZ, 4, 4, GROUP, FA), bf16),
            pltpu.VMEM((NZ, 16, GROUP, FC), bf16),
            pltpu.VMEM((NZ, 2 * WT, 2 * COLS), bf16),
            pltpu.VMEM((NZ, 2 * WR, 2 * COLS), bf16),
            pltpu.VMEM((8, GROUP, 128), jnp.float32),
            pltpu.VMEM((8, GROUP, 128), jnp.float32),
            pltpu.VMEM((3, 16, GROUP, 128), jnp.float32),
            pltpu.VMEM((ROWS, 2 * WT), bf16),
            pltpu.VMEM((ROWS, 2 * WR), bf16),
            pltpu.VMEM((ROWS, 2 * WT), bf16),
            pltpu.VMEM((ROWS, 2 * WR), bf16),
            pltpu.VMEM((ROWS, 2 * COLS), jnp.float32),
            pltpu.VMEM((ROWS, 2 * COLS), jnp.float32),
            pltpu.SemaphoreType.DMA((NZ, NA + 1)),
            pltpu.SemaphoreType.DMA((NZ, 4)),
        ],
        compiler_params=pltpu.CompilerParams(vmem_limit_bytes=54 * 2**20),
        name="heads",
    )(*operands)


def local(hidden_t, gain_t, head_t, hidden_r, gain_r, head_r):
    xl, y, core, z, xh = (lax.axis_index(name) for name in AXES)
    x = 2 * xh + xl

    head_r_other = send(head_r, other_core)
    head_t_other = send(head_t, other_core)
    second_r = jnp.concatenate([hidden_t[:, FA:], hidden_r], axis=1)[None]
    first_t = hidden_t[None, :, :FA]
    for x_core, step in ((0, 0), (0, 1), (1, 0)):
        got_r = send(second_r, pair_x_or_y(PAIRS4[step], x_core))
        got_t = send(first_t, pair_z(PAIRS8[2 * x_core + step]))
        second_r = jnp.concatenate([second_r, got_r])
        first_t = jnp.concatenate([first_t, got_t])
        second_r, first_t = lax.optimization_barrier((second_r, first_t))
    first_t = after(first_t, head_r_other, head_t_other)[None]
    before, behind = send(first_t, x_or_y(1, 1)), send(first_t, x_or_y(-1, 1))
    got_r = send(second_r, pair_x_or_y(PAIRS4[1], 1))
    second_r = jnp.concatenate([second_r, got_r])
    one_t = jnp.concatenate([first_t, before])
    one_t, before = lax.optimization_barrier((one_t, before, behind, got_r))[:2]
    two_t = jnp.concatenate([behind, send(before, x_or_y(1, 1))])
    blocks_c = ring8(second_r, core)
    low_one, high_one = send(one_t, x_or_y(1, 0)), send(one_t, x_or_y(-1, 0))
    ready_t = after(two_t, low_one, high_one, *blocks_c[1:3])
    low_two, high_two = send(ready_t, x_or_y(1, 0)), send(ready_t, x_or_y(-1, 0))
    far_one = send(after(low_one, low_two, high_two), x_or_y(1, 0))
    far_two = send(after(high_two, low_two), x_or_y(-1, 0))
    blocks_a = [one_t, two_t, low_one, low_two, high_one, high_two, far_one, far_two]

    ring = jnp.array((0, -1, 1, 2), jnp.int32)
    zeros = jnp.zeros((4, 4), jnp.int32)
    last, middle = zeros + ring[:, None], zeros + ring[None, :]
    on_x = core == 0
    xa = (x + jnp.where(on_x, last, middle)) % NX
    ya = (y + jnp.where(on_x, middle, last)) % NY
    in_x = zeros + jnp.where(on_x, jnp.array(sources(PAIRS4))[x][None, :], jnp.array(sources(PAIRS4))[x][:, None])
    in_y = zeros + jnp.where(on_x, jnp.array(sources(PAIRS4))[y][:, None], jnp.array(sources(PAIRS4))[y][None, :])
    xc, yc = in_x, in_y
    zs_c = (z + jnp.array(RING8, jnp.int32)) % NZ
    zs_a = jnp.array(sources(PAIRS8))[z]
    table = jnp.concatenate(
        [
            ((xa % 2) * NY + ya).reshape(16),
            (xa // 2).reshape(16),
            zs_c,
            ((xc % 2) * NY + yc).reshape(16),
            (xc // 2).reshape(16),
            jnp.argmax(zs_a[None, :] == zs_c[:, None], axis=1),
        ]
    ).astype(jnp.int32)

    wide_gain_t = gain_t.astype(jnp.float32).reshape(16, 1, WT)
    wide_gain_r = gain_r.astype(jnp.float32).reshape(16, 1, WR)
    logits, logits_cross, stats = heads_call(
        table,
        wide_gain_t, wide_gain_r,
        *blocks_a, *blocks_c,
        head_t.reshape(NZ, 2 * WT, COLS), head_t_other.reshape(NZ, 2 * WT, COLS),
        head_r.reshape(NZ, 2 * WR, COLS), head_r_other.reshape(NZ, 2 * WR, COLS),
    )

    logits_other = send(logits_cross, other_core)
    for pair, steps in ((pair_x, PAIRS4), (pair_y, PAIRS4), (pair_z, PAIRS8)):
        for partner in steps:
            stats = merge([stats, send(stats, pair(partner))])
    stats_other = send(stats, other_core)

    out = pl.pallas_call(
        contrast_kernel,
        out_shape=jax.ShapeDtypeStruct((8, 2, GROUP, COLS), jnp.float32),
        in_specs=[smem] + [vmem] * 4,
        out_specs=vmem,
        name="contrast",
    )(core.astype(jnp.int32).reshape(1), stats, stats_other, logits, logits_other)
    return out.reshape(2 * ROWS, COLS)


def solution(mesh):
    fine = Mesh(np.asarray(mesh.devices).reshape(SIZES), AXES)
    rows, features, vocabulary = ("xl", "y", "core"), ("z", "xh"), AXES
    placed = (
        P(rows, features),
        P(),
        P(None, vocabulary),
        P(rows, features),
        P(),
        P(None, vocabulary),
    )
    return jax.shard_map(
        local, mesh=fine, in_specs=placed, out_specs=P(None, vocabulary), check_vma=False
    )
```

time: 409 us -> 156 us (0.38)
  blocking collectives: 193 us -> 0 us
  waiting for transfers between devices: 170 us -> 51.3 us
  starting transfers between devices: 0.08 us -> 64.9 us
  Pallas kernels: 0 us -> 20.9 us
  matrix products: 17.4 us -> 0 us
  between operations: 13.1 us -> 0.24 us
  local copies, waits for them, and re-layouts: 2.04 us -> 9.31 us
    all_gather x3 -> x0, waiting for transfers between devices: 170 us -> none  [the longest x1 89.3 us: local(): lax.all_gather(wide_t, 'dp', axis=0, tiled=True)]
    pmax x1 -> x0, blocking collectives: 77 us -> none  [local(): peak_t, peak_r = lax.pmax((local_peak_t, local_peak_r), ('dp', 'tensor'))]
    psum x1 -> x0, blocking collectives: 73.6 us -> none  [local(): lax.psum((local_total_t, local_total_r), ('dp', 'tensor'))]
    ppermute x0 -> x34, starting transfers between devices: none -> 64.9 us  [send(): return lax.ppermute(value, AXES, pairs)]
    ppermute x0 -> x34, waiting for transfers between devices: none -> 51.3 us  [send(): return lax.ppermute(value, AXES, pairs)]
    all_gather x1 -> x0, blocking collectives: 42.1 us -> none  [local(): lax.all_gather(reference_hidden, 'tensor', axis=1, tiled=True)]
    pallas_call x0 -> x2, Pallas kernels: none -> 20.9 us  [the longest x1 18.3 us: heads_call(): pl.pallas_call(heads_kernel, out_shape=[square] * 2 + [jax.ShapeDtypeStru...]
    dot_general x2 -> x0, matrix products: 17.4 us -> none  [the longest x1 13.6 us: local(): jnp.dot(normalize_full(lax.all_gather(wide_t, 'dp', axis=0, tiled=True),...]
  transfers between devices with their start and end apart: 3 -> 34, of which waited for: 3 -> 19; matrix products, arithmetic and copies ran while one was open for 2% -> 10% of each run, Pallas kernels for 0% -> 0%
where the time goes in v1:
time: 156 us
  starting transfers between devices  64.9 us (42%)
  waiting for transfers between devices  51.3 us (33%)
  Pallas kernels  20.9 us (13%)
  local copies, waits for them, and re-layouts  9.31 us (6%)
  other arithmetic  9.14 us (6%)
    ppermute x34, starting transfers between devices, send(): return lax.ppermute(value, AXES, pairs)  64.9 us
    ppermute x34, waiting for transfers between devices, send(): return lax.ppermute(value, AXES, pairs)  51.3 us
    pallas_call x1, Pallas kernels, heads_call(): pl.pallas_call(heads_kernel, out_shape=[square] * 2 + [jax.ShapeDtypeStru...  18.3 us
    unnamed x20, local copies, waits for them, and re-layouts  3.44 us
  transfers between devices with their start and end apart: 34, of which 19 were waited for; matrix products, arithmetic and copies ran while one was open for 10% of the time, Pallas kernels for 0%

profile of v1, /device:TPU:1, one launch (start us, length us, event | category | flops | bytes accessed | tf_op | source)
XLA Modules:
  0.0 155.8 jit_solution(12847116294904083462)
XLA Ops:
  0.0 3.2 %collective-permute-start.7 = (bf16[16384,256]{1,0:T(8,128)(2,1)}, bf16[16384,256]{1,0:T(8,128)(2,1)}, u32[]{:S(2)}, u32[]{:S(2)}) collective-permute-start(bf16[16384,256]{1,0:T(8,128)(2,1)} %param.15), channel_id=1, source_target_pairs={{0,16},{1,17},{2,18},{3,19},{4,20},{5,21},{6,22},{7,23},{8,24},{9,... | collective-permute-start | bytes 25165832 | tf_op jit(solution)/shard_map/ppermute | solution.py:40
  10.3 5.4 %collective-permute-start.3 = (bf16[2,32,896]{2,1,0:T(8,128)(2,1)S(1)}, bf16[2,32,896]{2,1,0:T(8,128)(2,1)S(1)}, u32[]{:S(2)}, u32[]{:S(2)}) collective-permute-start(bf16[2,32,896]{2,1,0:T(8,128)(2,1)S(1)} %pad_maximum_fusion.4), channel_id=1, source_target_pairs={{0,14},{1,15},{2,4},{3,5},{4,2},{5,3},{6,8},{7,9},{8,6},{9,7},{10,... | collective-permute-start | bytes 344072 | tf_op jit(solution)/shard_map/ppermute | solution.py:40
  23.1 8.1 %collective-permute-done.5 = bf16[4,32,896]{2,1,0:T(8,128)(2,1)S(1)} collective-permute-done((bf16[4,32,896]{2,1,0:T(8,128)(2,1)S(1)}, bf16[4,32,896]{2,1,0:T(8,128)(2,1)S(1)}, u32[]{:S(2)}, u32[]{:S(2)}) %collective-permute-start.5) | collective-permute-done | bytes 229408 | tf_op jit(solution)/shard_map/ppermute | solution.py:40
  37.1 4.8 %collective-permute-done.8 = bf16[1,8,32,896]{3,2,1,0:T(8,128)(2,1)} collective-permute-done((bf16[1,8,32,896]{3,2,1,0:T(8,128)(2,1)S(1)}, bf16[1,8,32,896]{3,2,1,0:T(8,128)(2,1)}, u32[]{:S(2)}, u32[]{:S(2)}) %collective-permute-start.8) | collective-permute-done | bytes 458784 | tf_op jit(solution)/shard_map/ppermute | solution.py:40
  44.0 2.7 %collective-permute-start.13 = (bf16[2,8,32,896]{3,2,1,0:T(8,128)(2,1)S(1)}, bf16[2,8,32,896]{3,2,1,0:T(8,128)(2,1)}, u32[]{:S(2)}, u32[]{:S(2)}) collective-permute-start(bf16[2,8,32,896]{3,2,1,0:T(8,128)(2,1)S(1)} %pad_maximum_fusion.refs_3_), channel_id=1, source_target_pairs={{0,129},{1,128},{2,131},{3,130},{4,133},{5,132},{6,135},{7,134},{8... | collective-permute-start | bytes 2752520 | tf_op jit(solution)/shard_map/ppermute | solution.py:40
  48.3 2.7 %collective-permute-start.15 = (bf16[16,32,384]{2,1,0:T(8,128)(2,1)S(1)}, bf16[16,32,384]{2,1,0:T(8,128)(2,1)}, u32[]{:S(2)}, u32[]{:S(2)}) collective-permute-start(bf16[16,32,384]{2,1,0:T(8,128)(2,1)S(1)} %constant_dynamic-update-slice_fusion.2.refs_11_), channel_id=1, source_target_pairs={{0,14},{1,15},{2,0},{3,1},{4,2},{5,3},{6,4},{7,5},{8,6},{9,7},{10,... | collective-permute-start | bytes 1179656 | tf_op jit(solution)/shard_map/ppermute | solution.py:40
  53.6 7.2 %collective-permute-done.11 = bf16[1,8,32,896]{3,2,1,0:T(8,128)(2,1)} collective-permute-done((bf16[1,8,32,896]{3,2,1,0:T(8,128)(2,1)}, bf16[1,8,32,896]{3,2,1,0:T(8,128)(2,1)}, u32[]{:S(2)}, u32[]{:S(2)}) %collective-permute-start.11) | collective-permute-done | bytes 458784 | tf_op jit(solution)/shard_map/ppermute | solution.py:40
  62.8 2.7 %collective-permute-start.17 = (bf16[2,8,32,896]{3,2,1,0:T(8,128)(2,1)}, bf16[2,8,32,896]{3,2,1,0:T(8,128)(2,1)}, u32[]{:S(2)}, u32[]{:S(2)}) collective-permute-start(bf16[2,8,32,896]{3,2,1,0:T(8,128)(2,1)} %constant_dynamic-update-slice_fusion.refs_4_), channel_id=1, source_target_pairs={{0,129},{1,128},{2,131},{3,130},{4,133},{5,132},{6,135},{7,134},{8... | collective-permute-start | bytes 2752520 | tf_op jit(solution)/shard_map/ppermute | solution.py:40
  65.5 2.7 %collective-permute-start.21 = (bf16[16,32,384]{2,1,0:T(8,128)(2,1)}, bf16[16,32,384]{2,1,0:T(8,128)(2,1)}, u32[]{:S(2)}, u32[]{:S(2)}) collective-permute-start(bf16[16,32,384]{2,1,0:T(8,128)(2,1)} %collective-permute-done.15.refs_13_), channel_id=1, source_target_pairs={{0,14},{1,15},{2,0},{3,1},{4,2},{5,3},{6,4},{7,5},{8,6},{9,7},{10,... | collective-permute-start | bytes 1179656 | tf_op jit(solution)/shard_map/ppermute | solution.py:40
  74.8 2.7 %collective-permute-start.23 = (bf16[16,32,384]{2,1,0:T(8,128)(2,1)}, bf16[16,32,384]{2,1,0:T(8,128)(2,1)S(1)}, u32[]{:S(2)}, u32[]{:S(2)}) collective-permute-start(bf16[16,32,384]{2,1,0:T(8,128)(2,1)} %collective-permute-done.21.refs_15_), channel_id=1, source_target_pairs={{0,14},{1,15},{2,0},{3,1},{4,2},{5,3},{6,4},{7,5},{8,6},{9,7},{10,... | collective-permute-start | bytes 1179656 | tf_op jit(solution)/shard_map/ppermute | solution.py:40
  79.5 3.3 %collective-permute-done.22.refs_16_ = bf16[16,32,384]{2,1,0:T(8,128)(2,1)S(1)} collective-permute-done((bf16[16,32,384]{2,1,0:T(8,128)(2,1)}, bf16[16,32,384]{2,1,0:T(8,128)(2,1)S(1)}, u32[]{:S(2)}, u32[]{:S(2)}) %collective-permute-start.22) | collective-permute-done | bytes 393248 | tf_op jit(solution)/shard_map/ppermute | solution.py:40
  84.5 2.6 %collective-permute-start.24 = (bf16[16,32,384]{2,1,0:T(8,128)(2,1)}, bf16[16,32,384]{2,1,0:T(8,128)(2,1)}, u32[]{:S(2)}, u32[]{:S(2)}) collective-permute-start(bf16[16,32,384]{2,1,0:T(8,128)(2,1)} %broadcast_select_fusion), channel_id=1, source_target_pairs={{0,2},{1,3},{2,4},{3,5},{4,6},{5,7},{6,8},{7,9},{8,10},{9,11},{10,... | collective-permute-start | bytes 1179656 | tf_op jit(solution)/shard_map/ppermute | solution.py:40
  89.1 3.1 %collective-permute-done.24.refs_18_ = bf16[16,32,384]{2,1,0:T(8,128)(2,1)} collective-permute-done((bf16[16,32,384]{2,1,0:T(8,128)(2,1)}, bf16[16,32,384]{2,1,0:T(8,128)(2,1)}, u32[]{:S(2)}, u32[]{:S(2)}) %collective-permute-start.24) | collective-permute-done | bytes 393248 | tf_op jit(solution)/shard_map/ppermute | solution.py:40
  93.6 18.3 %heads.1 = (f32[2,256,256]{2,1,0:T(8,128)}, f32[2,256,256]{2,1,0:T(8,128)}, f32[8,256]{1,0:T(8,128)}) custom-call(s32[80]{0:T(128)} %concatenate.54.refs_0_, f32[16,1,1024]{2,1,0:T(1,128)} %bitcast.25, f32[16,1,256]{2,1,0:T(1,128)} %bitcast.26, bf16[2,8,32,896]{3,2,1,0:T(8,128)(2,1)} %copy-done, ...), custom_call_target="tpu_custom_call" | custom-call | tf_op jit(solution)/shard_map/heads/pallas_call | solution.py:282
  111.9 3.7 %collective-permute-start.25 = (f32[8,256]{1,0:T(8,128)}, f32[8,256]{1,0:T(8,128)S(1)}, u32[]{:S(2)}, u32[]{:S(2)}) collective-permute-start(f32[8,256]{1,0:T(8,128)} %get-tuple-element.34), channel_id=1, source_target_pairs={{0,128},{1,129},{2,130},{3,131},{4,132},{5,133},{6,134},{7,135},{8... | collective-permute-start | bytes 24584 | tf_op jit(solution)/shard_map/ppermute | solution.py:40
  117.7 2.4 %collective-permute-start.26 = (f32[8,256]{1,0:T(8,128)S(1)}, f32[8,256]{1,0:T(8,128)S(1)}, u32[]{:S(2)}, u32[]{:S(2)}) collective-permute-start(f32[8,256]{1,0:T(8,128)S(1)} %maximum_maximum_fusion), channel_id=1, source_target_pairs={{0,129},{1,128},{2,131},{3,130},{4,133},{5,132},{6,135},{7,134},{8... | collective-permute-start | bytes 24584 | tf_op jit(solution)/shard_map/ppermute | solution.py:40
  121.6 2.5 %collective-permute-done.27 = f32[8,256]{1,0:T(8,128)S(1)} collective-permute-done((f32[8,256]{1,0:T(8,128)S(1)}, f32[8,256]{1,0:T(8,128)S(1)}, u32[]{:S(2)}, u32[]{:S(2)}) %collective-permute-start.27) | collective-permute-done | bytes 8224 | tf_op jit(solution)/shard_map/ppermute | solution.py:40
  124.2 3.7 %collective-permute-done.28 = f32[8,256]{1,0:T(8,128)S(1)} collective-permute-done((f32[8,256]{1,0:T(8,128)S(1)}, f32[8,256]{1,0:T(8,128)S(1)}, u32[]{:S(2)}, u32[]{:S(2)}) %collective-permute-start.28) | collective-permute-done | bytes 8224 | tf_op jit(solution)/shard_map/ppermute | solution.py:40
  128.0 2.5 %collective-permute-done.29 = f32[8,256]{1,0:T(8,128)S(1)} collective-permute-done((f32[8,256]{1,0:T(8,128)S(1)}, f32[8,256]{1,0:T(8,128)S(1)}, u32[]{:S(2)}, u32[]{:S(2)}) %collective-permute-start.29) | collective-permute-done | bytes 8224 | tf_op jit(solution)/shard_map/ppermute | solution.py:40
  130.6 3.4 %collective-permute-start.30 = (f32[8,256]{1,0:T(8,128)S(1)}, f32[8,256]{1,0:T(8,128)S(1)}, u32[]{:S(2)}, u32[]{:S(2)}) collective-permute-start(f32[8,256]{1,0:T(8,128)S(1)} %maximum_maximum_fusion.4), channel_id=1, source_target_pairs={{0,14},{1,15},{2,4},{3,5},{4,2},{5,3},{6,8},{7,9},{8,6},{9,7},{10,... | collective-permute-start | bytes 24584 | tf_op jit(solution)/shard_map/ppermute | solution.py:40
  134.0 8.7 %collective-permute-start.33 = (f32[2,256,256]{2,1,0:T(8,128)}, f32[2,256,256]{2,1,0:T(8,128)S(1)}, u32[]{:S(2)}, u32[]{:S(2)}) collective-permute-start(f32[2,256,256]{2,1,0:T(8,128)} %get-tuple-element.36), channel_id=1, source_target_pairs={{0,16},{1,17},{2,18},{3,19},{4,20},{5,21},{6,22},{7,23},{8,24},{9,... | collective-permute-start | bytes 1572872 | tf_op jit(solution)/shard_map/ppermute | solution.py:40
  142.8 2.3 %collective-permute-start.31 = (f32[8,256]{1,0:T(8,128)S(1)}, f32[8,256]{1,0:T(8,128)S(1)}, u32[]{:S(2)}, u32[]{:S(2)}) collective-permute-start(f32[8,256]{1,0:T(8,128)S(1)} %maximum_maximum_fusion.5), channel_id=1, source_target_pairs={{0,6},{1,7},{2,12},{3,13},{4,10},{5,11},{6,0},{7,1},{8,14},{9,15},... | collective-permute-start | bytes 24584 | tf_op jit(solution)/shard_map/ppermute | solution.py:40
  147.2 4.3 %collective-permute-start.32 = (f32[8,256]{1,0:T(8,128)S(1)}, f32[8,256]{1,0:T(8,128)S(1)}, u32[]{:S(2)}, u32[]{:S(2)}) collective-permute-start(f32[8,256]{1,0:T(8,128)S(1)} %maximum_maximum_fusion.6.own_ref), channel_id=1, source_target_pairs={{0,16},{1,17},{2,18},{3,19},{4,20},{5,21},{6,22},{7,23},{8,24},{9,... | collective-permute-start | bytes 24584 | tf_op jit(solution)/shard_map/ppermute | solution.py:40
  153.1 2.6 %contrast.1 = f32[8,2,32,256]{3,2,1,0:T(8,128)} custom-call(s32[1]{0:T(128)} %bitcast.core_ref, f32[8,256]{1,0:T(8,128)} %copy-done.7, f32[8,256]{1,0:T(8,128)} %copy-done.8, f32[2,256,256]{2,1,0:T(8,128)} %get-tuple-element.35.logits_own, f32[2,256,256]{2,1,0:T(8,128)} %copy-done.5), custom_call_target="tpu_custom_call" | custom-call | tf_op jit(solution)/shard_map/contrast/pallas_call | solution.py:376
  (111 shorter events, 49.9 us)
Async XLA Ops:
  0.0 31.3 %collective-permute-start.7 = (bf16[16384,256]{1,0:T(8,128)(2,1)}, bf16[16384,256]{1,0:T(8,128)(2,1)}, u32[]{:S(2)}, u32[]{:S(2)}) collective-permute-start(bf16[16384,256]{1,0:T(8,128)(2,1)} %param.15), channel_id=1, source_target_pairs={{0,16},{1,17},{2,18},{3,19},{4,20},{5,21},{6,22},{7,23},{8,24},{9,... | collective-permute-start | bytes 25165832 | tf_op jit(solution)/shard_map/ppermute | solution.py:40
  3.2 28.0 %collective-permute-start.6 = (bf16[4096,256]{1,0:T(8,128)(2,1)}, bf16[4096,256]{1,0:T(8,128)(2,1)S(1)}, u32[]{:S(2)}, u32[]{:S(2)}) collective-permute-start(bf16[4096,256]{1,0:T(8,128)(2,1)} %param.18), channel_id=1, source_target_pairs={{0,16},{1,17},{2,18},{3,19},{4,20},{5,21},{6,22},{7,23},{8,24},{9,... | collective-permute-start | bytes 6291464 | tf_op jit(solution)/shard_map/ppermute | solution.py:40
  8.6 7.0 %collective-permute-start.2 = (bf16[2,32,384]{2,1,0:T(8,128)(2,1)S(1)}, bf16[2,32,384]{2,1,0:T(8,128)(2,1)S(1)}, u32[]{:S(2)}, u32[]{:S(2)}) collective-permute-start(bf16[2,32,384]{2,1,0:T(8,128)(2,1)S(1)} %pad_maximum_fusion.6), channel_id=1, source_target_pairs={{0,129},{1,128},{2,131},{3,130},{4,133},{5,132},{6,135},{7,134},{8... | collective-permute-start | bytes 147464 | tf_op jit(solution)/shard_map/ppermute | solution.py:40
  10.3 7.6 %collective-permute-start.3 = (bf16[2,32,896]{2,1,0:T(8,128)(2,1)S(1)}, bf16[2,32,896]{2,1,0:T(8,128)(2,1)S(1)}, u32[]{:S(2)}, u32[]{:S(2)}) collective-permute-start(bf16[2,32,896]{2,1,0:T(8,128)(2,1)S(1)} %pad_maximum_fusion.4), channel_id=1, source_target_pairs={{0,14},{1,15},{2,4},{3,5},{4,2},{5,3},{6,8},{7,9},{8,6},{9,7},{10,... | collective-permute-start | bytes 344072 | tf_op jit(solution)/shard_map/ppermute | solution.py:40
  17.9 13.3 %collective-permute-start.5 = (bf16[4,32,896]{2,1,0:T(8,128)(2,1)S(1)}, bf16[4,32,896]{2,1,0:T(8,128)(2,1)S(1)}, u32[]{:S(2)}, u32[]{:S(2)}) collective-permute-start(bf16[4,32,896]{2,1,0:T(8,128)(2,1)S(1)} %pad_maximum_fusion.2), channel_id=1, source_target_pairs={{0,6},{1,7},{2,12},{3,13},{4,10},{5,11},{6,0},{7,1},{8,14},{9,15},... | collective-permute-start | bytes 688136 | tf_op jit(solution)/shard_map/ppermute | solution.py:40
  31.3 10.7 %collective-permute-start.8 = (bf16[1,8,32,896]{3,2,1,0:T(8,128)(2,1)S(1)}, bf16[1,8,32,896]{3,2,1,0:T(8,128)(2,1)}, u32[]{:S(2)}, u32[]{:S(2)}) collective-permute-start(bf16[1,8,32,896]{3,2,1,0:T(8,128)(2,1)S(1)} %bitcast.22), channel_id=1, source_target_pairs={{0,32},{1,33},{2,34},{3,35},{4,36},{5,37},{6,38},{7,39},{8,40},{9,... | collective-permute-start | bytes 1376264 | tf_op jit(solution)/shard_map/ppermute | solution.py:40
  33.6 10.4 %collective-permute-start.9 = (bf16[1,8,32,896]{3,2,1,0:T(8,128)(2,1)S(1)}, bf16[1,8,32,896]{3,2,1,0:T(8,128)(2,1)S(1)}, u32[]{:S(2)}, u32[]{:S(2)}) collective-permute-start(bf16[1,8,32,896]{3,2,1,0:T(8,128)(2,1)S(1)} %bitcast.23), channel_id=1, source_target_pairs={{0,96},{1,97},{2,98},{3,99},{4,100},{5,101},{6,102},{7,103},{8,104... | collective-permute-start | bytes 1376264 | tf_op jit(solution)/shard_map/ppermute | solution.py:40
  35.8 8.2 %collective-permute-start.10 = (bf16[8,32,384]{2,1,0:T(8,128)(2,1)S(1)}, bf16[8,32,384]{2,1,0:T(8,128)(2,1)S(1)}, u32[]{:S(2)}, u32[]{:S(2)}) collective-permute-start(bf16[8,32,384]{2,1,0:T(8,128)(2,1)S(1)} %pad_maximum_fusion.3), channel_id=1, source_target_pairs={{0,96},{1,97},{2,98},{3,99},{4,100},{5,101},{6,102},{7,103},{8,104... | collective-permute-start | bytes 589832 | tf_op jit(solution)/shard_map/ppermute | solution.py:40
  43.9 18.8 %collective-permute-start.12 = (bf16[2,8,32,896]{3,2,1,0:T(8,128)(2,1)S(1)}, bf16[2,8,32,896]{3,2,1,0:T(8,128)(2,1)}, u32[]{:S(2)}, u32[]{:S(2)}) collective-permute-start(bf16[2,8,32,896]{3,2,1,0:T(8,128)(2,1)S(1)} %pad_maximum_fusion.refs_3_), channel_id=1, source_target_pairs={{0,128},{1,129},{2,130},{3,131},{4,132},{5,133},{6,134},{7,135},{8... | collective-permute-start | bytes 2752520 | tf_op jit(solution)/shard_map/ppermute | solution.py:40
  44.0 18.8 %collective-permute-start.13 = (bf16[2,8,32,896]{3,2,1,0:T(8,128)(2,1)S(1)}, bf16[2,8,32,896]{3,2,1,0:T(8,128)(2,1)}, u32[]{:S(2)}, u32[]{:S(2)}) collective-permute-start(bf16[2,8,32,896]{3,2,1,0:T(8,128)(2,1)S(1)} %pad_maximum_fusion.refs_3_), channel_id=1, source_target_pairs={{0,129},{1,128},{2,131},{3,130},{4,133},{5,132},{6,135},{7,134},{8... | collective-permute-start | bytes 2752520 | tf_op jit(solution)/shard_map/ppermute | solution.py:40
  46.6 14.2 %collective-permute-start.11 = (bf16[1,8,32,896]{3,2,1,0:T(8,128)(2,1)}, bf16[1,8,32,896]{3,2,1,0:T(8,128)(2,1)}, u32[]{:S(2)}, u32[]{:S(2)}) collective-permute-start(bf16[1,8,32,896]{3,2,1,0:T(8,128)(2,1)} %collective-permute-done.8), channel_id=1, source_target_pairs={{0,32},{1,33},{2,34},{3,35},{4,36},{5,37},{6,38},{7,39},{8,40},{9,... | collective-permute-start | bytes 1376264 | tf_op jit(solution)/shard_map/ppermute | solution.py:40
  48.2 14.4 %collective-permute-start.14 = (bf16[16,32,384]{2,1,0:T(8,128)(2,1)S(1)}, bf16[16,32,384]{2,1,0:T(8,128)(2,1)}, u32[]{:S(2)}, u32[]{:S(2)}) collective-permute-start(bf16[16,32,384]{2,1,0:T(8,128)(2,1)S(1)} %constant_dynamic-update-slice_fusion.2.refs_11_), channel_id=1, source_target_pairs={{0,2},{1,3},{2,4},{3,5},{4,6},{5,7},{6,8},{7,9},{8,10},{9,11},{10,... | collective-permute-start | bytes 1179656 | tf_op jit(solution)/shard_map/ppermute | solution.py:40
  48.3 14.4 %collective-permute-start.15 = (bf16[16,32,384]{2,1,0:T(8,128)(2,1)S(1)}, bf16[16,32,384]{2,1,0:T(8,128)(2,1)}, u32[]{:S(2)}, u32[]{:S(2)}) collective-permute-start(bf16[16,32,384]{2,1,0:T(8,128)(2,1)S(1)} %constant_dynamic-update-slice_fusion.2.refs_11_), channel_id=1, source_target_pairs={{0,14},{1,15},{2,0},{3,1},{4,2},{5,3},{6,4},{7,5},{8,6},{9,7},{10,... | collective-permute-start | bytes 1179656 | tf_op jit(solution)/shard_map/ppermute | solution.py:40
  62.7 14.8 %collective-permute-start.16 = (bf16[2,8,32,896]{3,2,1,0:T(8,128)(2,1)}, bf16[2,8,32,896]{3,2,1,0:T(8,128)(2,1)}, u32[]{:S(2)}, u32[]{:S(2)}) collective-permute-start(bf16[2,8,32,896]{3,2,1,0:T(8,128)(2,1)} %constant_dynamic-update-slice_fusion.refs_4_), channel_id=1, source_target_pairs={{0,128},{1,129},{2,130},{3,131},{4,132},{5,133},{6,134},{7,135},{8... | collective-permute-start | bytes 2752520 | tf_op jit(solution)/shard_map/ppermute | solution.py:40
  62.8 14.7 %collective-permute-start.17 = (bf16[2,8,32,896]{3,2,1,0:T(8,128)(2,1)}, bf16[2,8,32,896]{3,2,1,0:T(8,128)(2,1)}, u32[]{:S(2)}, u32[]{:S(2)}) collective-permute-start(bf16[2,8,32,896]{3,2,1,0:T(8,128)(2,1)} %constant_dynamic-update-slice_fusion.refs_4_), channel_id=1, source_target_pairs={{0,129},{1,128},{2,131},{3,130},{4,133},{5,132},{6,135},{7,134},{8... | collective-permute-start | bytes 2752520 | tf_op jit(solution)/shard_map/ppermute | solution.py:40
  65.5 9.3 %collective-permute-start.20 = (bf16[16,32,384]{2,1,0:T(8,128)(2,1)}, bf16[16,32,384]{2,1,0:T(8,128)(2,1)}, u32[]{:S(2)}, u32[]{:S(2)}) collective-permute-start(bf16[16,32,384]{2,1,0:T(8,128)(2,1)} %collective-permute-done.14.refs_12_), channel_id=1, source_target_pairs={{0,2},{1,3},{2,4},{3,5},{4,6},{5,7},{6,8},{7,9},{8,10},{9,11},{10,... | collective-permute-start | bytes 1179656 | tf_op jit(solution)/shard_map/ppermute | solution.py:40
  65.5 9.3 %collective-permute-start.21 = (bf16[16,32,384]{2,1,0:T(8,128)(2,1)}, bf16[16,32,384]{2,1,0:T(8,128)(2,1)}, u32[]{:S(2)}, u32[]{:S(2)}) collective-permute-start(bf16[16,32,384]{2,1,0:T(8,128)(2,1)} %collective-permute-done.15.refs_13_), channel_id=1, source_target_pairs={{0,14},{1,15},{2,0},{3,1},{4,2},{5,3},{6,4},{7,5},{8,6},{9,7},{10,... | collective-permute-start | bytes 1179656 | tf_op jit(solution)/shard_map/ppermute | solution.py:40
  74.8 8.0 %collective-permute-start.22 = (bf16[16,32,384]{2,1,0:T(8,128)(2,1)}, bf16[16,32,384]{2,1,0:T(8,128)(2,1)S(1)}, u32[]{:S(2)}, u32[]{:S(2)}) collective-permute-start(bf16[16,32,384]{2,1,0:T(8,128)(2,1)} %collective-permute-done.20.refs_14_), channel_id=1, source_target_pairs={{0,2},{1,3},{2,4},{3,5},{4,6},{5,7},{6,8},{7,9},{8,10},{9,11},{10,... | collective-permute-start | bytes 1179656 | tf_op jit(solution)/shard_map/ppermute | solution.py:40
  74.8 8.0 %collective-permute-start.23 = (bf16[16,32,384]{2,1,0:T(8,128)(2,1)}, bf16[16,32,384]{2,1,0:T(8,128)(2,1)S(1)}, u32[]{:S(2)}, u32[]{:S(2)}) collective-permute-start(bf16[16,32,384]{2,1,0:T(8,128)(2,1)} %collective-permute-done.21.refs_15_), channel_id=1, source_target_pairs={{0,14},{1,15},{2,0},{3,1},{4,2},{5,3},{6,4},{7,5},{8,6},{9,7},{10,... | collective-permute-start | bytes 1179656 | tf_op jit(solution)/shard_map/ppermute | solution.py:40
  77.6 14.6 %collective-permute-start.19 = (bf16[2,8,32,896]{3,2,1,0:T(8,128)(2,1)}, bf16[2,8,32,896]{3,2,1,0:T(8,128)(2,1)}, u32[]{:S(2)}, u32[]{:S(2)}) collective-permute-start(bf16[2,8,32,896]{3,2,1,0:T(8,128)(2,1)} %collective-permute-done.17.refs_8_), channel_id=1, source_target_pairs={{0,129},{1,128},{2,131},{3,130},{4,133},{5,132},{6,135},{7,134},{8... | collective-permute-start | bytes 2752520 | tf_op jit(solution)/shard_map/ppermute | solution.py:40
  79.5 14.1 %collective-permute-start.18 = (bf16[2,8,32,896]{3,2,1,0:T(8,128)(2,1)}, bf16[2,8,32,896]{3,2,1,0:T(8,128)(2,1)}, u32[]{:S(2)}, u32[]{:S(2)}) collective-permute-start(bf16[2,8,32,896]{3,2,1,0:T(8,128)(2,1)} %collective-permute-done.12.refs_5_), channel_id=1, source_target_pairs={{0,128},{1,129},{2,130},{3,131},{4,132},{5,133},{6,134},{7,135},{8... | collective-permute-start | bytes 2752520 | tf_op jit(solution)/shard_map/ppermute | solution.py:40
  84.5 7.7 %collective-permute-start.24 = (bf16[16,32,384]{2,1,0:T(8,128)(2,1)}, bf16[16,32,384]{2,1,0:T(8,128)(2,1)}, u32[]{:S(2)}, u32[]{:S(2)}) collective-permute-start(bf16[16,32,384]{2,1,0:T(8,128)(2,1)} %broadcast_select_fusion), channel_id=1, source_target_pairs={{0,2},{1,3},{2,4},{3,5},{4,6},{5,7},{6,8},{7,9},{8,10},{9,11},{10,... | collective-permute-start | bytes 1179656 | tf_op jit(solution)/shard_map/ppermute | solution.py:40
  130.6 12.1 %collective-permute-start.30 = (f32[8,256]{1,0:T(8,128)S(1)}, f32[8,256]{1,0:T(8,128)S(1)}, u32[]{:S(2)}, u32[]{:S(2)}) collective-permute-start(f32[8,256]{1,0:T(8,128)S(1)} %maximum_maximum_fusion.4), channel_id=1, source_target_pairs={{0,14},{1,15},{2,4},{3,5},{4,2},{5,3},{6,8},{7,9},{8,6},{9,7},{10,... | collective-permute-start | bytes 24584 | tf_op jit(solution)/shard_map/ppermute | solution.py:40
  134.0 18.4 %collective-permute-start.33 = (f32[2,256,256]{2,1,0:T(8,128)}, f32[2,256,256]{2,1,0:T(8,128)S(1)}, u32[]{:S(2)}, u32[]{:S(2)}) collective-permute-start(f32[2,256,256]{2,1,0:T(8,128)} %get-tuple-element.36), channel_id=1, source_target_pairs={{0,16},{1,17},{2,18},{3,19},{4,20},{5,21},{6,22},{7,23},{8,24},{9,... | collective-permute-start | bytes 1572872 | tf_op jit(solution)/shard_map/ppermute | solution.py:40
  (19 other events, 196.1 us)

commit v2 on v1

--- a/solution.py
+++ b/solution.py
@@ -96,16 +96,49 @@
 
 A_SLOTS = ((0, 0, 2), (0, 2, 2), (1, 0, 2), (1, 2, 2), (2, 0, 2), (2, 2, 2), (3, 0, 2), (3, 2, 2))
 NA = len(A_SLOTS)
-AHEAD = 2
+EARLY = NZ // 2
+
+
+def head_copies(own, other, z, to, sems):
+    return [
+        pltpu.make_async_copy(own.at[z], to.at[0], sems.at[0]),
+        pltpu.make_async_copy(other.at[z], to.at[1], sems.at[1]),
+    ]
+
+
+def preload_kernel(table_ref, own_ref, other_ref, to_ref, sems):
+    copies = [
+        copy
+        for i in range(EARLY)
+        for copy in head_copies(own_ref, other_ref, table_ref[32 + i], to_ref.at[i], sems.at[i])
+    ]
+    for copy in copies:
+        copy.start()
+    for copy in copies:
+        copy.wait()
+
+
+def preload(table, own, other):
+    early = pl.pallas_call(
+        preload_kernel,
+        out_shape=pltpu.VMEM((EARLY, 2, 2 * WT, COLS), jnp.bfloat16),
+        in_specs=[smem] + [hbm] * 2,
+        out_specs=vmem,
+        scratch_shapes=[pltpu.SemaphoreType.DMA((EARLY, 2))],
+        compiler_params=pltpu.CompilerParams(vmem_limit_bytes=44 * 2**20),
+        name="preload",
+    )(table, own, other)
+    return pltpu.with_memory_space_constraint(early, pltpu.VMEM)
 
 
 def heads_kernel(*refs):
     table_ref, gain_t_ref, gain_r_ref = refs[:3]
     a_refs, c_refs, head_refs = refs[3 : 3 + NA], refs[3 + NA : 11 + NA], refs[11 + NA : 15 + NA]
     head_t_own, head_t_other, head_r_own, head_r_other = head_refs
-    logits_own, logits_cross, stats_ref = refs[15 + NA : 18 + NA]
-    buf_a, buf_c, buf_t, buf_r = refs[18 + NA : 22 + NA]
-    scale_t, scale_r, sums, left_t0, left_r0, left_t1, left_r1, sum_t, sum_r, sem_x, sem_h = refs[22 + NA :]
+    early_t = refs[15 + NA]
+    logits_own, logits_cross, stats_ref = refs[16 + NA : 19 + NA]
+    buf_a, buf_c, buf_t, buf_r = refs[19 + NA : 23 + NA]
+    scale_t, scale_r, sums, left_t0, left_r0, left_t1, left_r1, sum_t, sum_r, sem_x, sem_t, sem_r = refs[23 + NA :]
     lefts = ((left_t0, left_r0), (left_t1, left_r1))
 
     def hidden_copies(i, c_ref):
@@ -117,25 +150,19 @@
         out.append(pltpu.make_async_copy(c_ref, buf_c.at[i], sem_x.at[i, NA]))
         return out
 
-    def head_copies(i):
+    early, late = [], []
+    for i in range(NZ):
         z = table_ref[32 + i]
-        own, other = pl.ds(0, COLS), pl.ds(COLS, COLS)
-        return [
-            pltpu.make_async_copy(head_t_own.at[z], buf_t.at[i, :, own], sem_h.at[i, 0]),
-            pltpu.make_async_copy(head_t_other.at[z], buf_t.at[i, :, other], sem_h.at[i, 1]),
-            pltpu.make_async_copy(head_r_own.at[z], buf_r.at[i, :, own], sem_h.at[i, 2]),
-            pltpu.make_async_copy(head_r_other.at[z], buf_r.at[i, :, other], sem_h.at[i, 3]),
-        ]
-
+        wanted = early if i < EARLY else late
+        wanted += head_copies(head_r_own, head_r_other, z, buf_r.at[i], sem_r.at[i])
+        if i >= EARLY:
+            at = i - EARLY
+            wanted += head_copies(head_t_own, head_t_other, z, buf_t.at[at], sem_t.at[at])
     for i in range(NZ):
         for copy in hidden_copies(i, c_refs[i]):
             copy.start()
-    def start_heads(i):
-        for copy in head_copies(i):
-            copy.start()
-
-    for i in range(AHEAD):
-        start_heads(i)
+    for copy in early + late:
+        copy.start()
 
     sums[...] = jnp.zeros_like(sums)
 
@@ -192,38 +219,35 @@
     sum_t[...] = jnp.zeros_like(sum_t)
     sum_r[...] = jnp.zeros_like(sum_r)
 
-    def multiply(i, left):
+    def multiply(i, left, heads_t, first):
         left_t, left_r = left
-        sum_t[...] += jnp.dot(left_t[...], buf_t[i], preferred_element_type=jnp.float32)
-        sum_r[...] += jnp.dot(left_r[...], buf_r[i], preferred_element_type=jnp.float32)
-
-    def wait_heads(i):
-        for copy in head_copies(i):
-            copy.wait()
+        for rows, heads, total in (
+            (left_t, heads_t.at[i], sum_t),
+            (left_r, buf_r.at[first + i], sum_r),
+        ):
+            for slot in range(2):
+                at = pl.ds(slot * COLS, COLS)
+                total[:, at] += jnp.dot(rows[...], heads[slot], preferred_element_type=jnp.float32)
 
     place(0, lefts[0])
 
-    def pair_step(pair, carry):
-        i = pair * 2
-        wait_heads(i)
-
-        @pl.when(i + AHEAD < NZ)
-        def _():
-            start_heads(i + AHEAD)
-
-        place(i + 1, lefts[1])
-        multiply(i, lefts[0])
-        wait_heads(i + 1)
-
-        @pl.when(i + 1 + AHEAD < NZ)
-        def _():
-            start_heads(i + 1 + AHEAD)
-
-        place(jnp.minimum(i + 2, NZ - 1), lefts[0])
-        multiply(i + 1, lefts[1])
-        return carry
-
-    lax.fori_loop(0, NZ // 2, pair_step, 0)
+    def steps(first, heads_t):
+        def pair_step(pair, carry):
+            i = pair * 2
+            place(first + i + 1, lefts[1])
+            multiply(i, lefts[0], heads_t, first)
+            place(jnp.minimum(first + i + 2, NZ - 1), lefts[0])
+            multiply(i + 1, lefts[1], heads_t, first)
+            return carry
+
+        lax.fori_loop(0, EARLY // 2, pair_step, 0)
+
+    for copy in early:
+        copy.wait()
+    steps(0, early_t)
+    for copy in late:
+        copy.wait()
+    steps(EARLY, buf_t)
     for model, total in enumerate((sum_t, sum_r)):
         logits_own[model] = total[:, :COLS]
         logits_cross[model] = total[:, COLS:]
@@ -282,13 +306,13 @@
     return pl.pallas_call(
         heads_kernel,
         out_shape=[square] * 2 + [jax.ShapeDtypeStruct((8, ROWS), jnp.float32)],
-        in_specs=[smem] + [vmem] * 2 + [hbm] * (NA + 12),
+        in_specs=[smem] + [vmem] * 2 + [hbm] * (NA + 12) + [vmem],
         out_specs=[vmem] * 3,
         scratch_shapes=[
             pltpu.VMEM((NZ, 4, 4, GROUP, FA), bf16),
             pltpu.VMEM((NZ, 16, GROUP, FC), bf16),
-            pltpu.VMEM((NZ, 2 * WT, 2 * COLS), bf16),
-            pltpu.VMEM((NZ, 2 * WR, 2 * COLS), bf16),
+            pltpu.VMEM((NZ - EARLY, 2, 2 * WT, COLS), bf16),
+            pltpu.VMEM((NZ, 2, 2 * WR, COLS), bf16),
             pltpu.VMEM((8, GROUP, 128), jnp.float32),
             pltpu.VMEM((8, GROUP, 128), jnp.float32),
             pltpu.VMEM((3, 16, GROUP, 128), jnp.float32),
@@ -299,9 +323,10 @@
             pltpu.VMEM((ROWS, 2 * COLS), jnp.float32),
             pltpu.VMEM((ROWS, 2 * COLS), jnp.float32),
             pltpu.SemaphoreType.DMA((NZ, NA + 1)),
-            pltpu.SemaphoreType.DMA((NZ, 4)),
+            pltpu.SemaphoreType.DMA((NZ - EARLY, 2)),
+            pltpu.SemaphoreType.DMA((NZ, 2)),
         ],
-        compiler_params=pltpu.CompilerParams(vmem_limit_bytes=54 * 2**20),
+        compiler_params=pltpu.CompilerParams(vmem_limit_bytes=28 * 2**20),
         name="heads",
     )(*operands)
 
@@ -312,14 +337,22 @@
 
     head_r_other = send(head_r, other_core)
     head_t_other = send(head_t, other_core)
+    got_t = send(hidden_t[None], pair_z(PAIRS8[0]))[:, :, :FA]
     second_r = jnp.concatenate([hidden_t[:, FA:], hidden_r], axis=1)[None]
-    first_t = hidden_t[None, :, :FA]
-    for x_core, step in ((0, 0), (0, 1), (1, 0)):
-        got_r = send(second_r, pair_x_or_y(PAIRS4[step], x_core))
-        got_t = send(first_t, pair_z(PAIRS8[2 * x_core + step]))
-        second_r = jnp.concatenate([second_r, got_r])
-        first_t = jnp.concatenate([first_t, got_t])
-        second_r, first_t = lax.optimization_barrier((second_r, first_t))
+    got_r = send(second_r, pair_x_or_y(PAIRS4[0], 0))
+    second_r = jnp.concatenate([second_r, got_r])
+    first_t = jnp.concatenate([hidden_t[None, :, :FA], got_t])
+    second_r, first_t = lax.optimization_barrier((second_r, first_t))
+    got_t = send(first_t, pair_z(PAIRS8[1]))
+    got_r = send(second_r, pair_x_or_y(PAIRS4[1], 0))
+    second_r = jnp.concatenate([second_r, got_r])
+    second_r, got_t = lax.optimization_barrier((second_r, got_t))
+    near_t = send(got_t, pair_z(PAIRS8[0]))
+    next_t = send(got_t, lambda x, y, z, c: (x, y, PAIRS8[1][PAIRS8[0][z]], c))
+    got_r = send(second_r, pair_x_or_y(PAIRS4[0], 1))
+    second_r = jnp.concatenate([second_r, got_r])
+    first_t = jnp.concatenate([first_t, got_t, near_t, next_t])
+    second_r, first_t = lax.optimization_barrier((second_r, first_t))
     first_t = after(first_t, head_r_other, head_t_other)[None]
     before, behind = send(first_t, x_or_y(1, 1)), send(first_t, x_or_y(-1, 1))
     got_r = send(second_r, pair_x_or_y(PAIRS4[1], 1))
@@ -345,7 +378,9 @@
     in_y = zeros + jnp.where(on_x, jnp.array(sources(PAIRS4))[y][:, None], jnp.array(sources(PAIRS4))[y][None, :])
     xc, yc = in_x, in_y
     zs_c = (z + jnp.array(RING8, jnp.int32)) % NZ
-    zs_a = jnp.array(sources(PAIRS8))[z]
+    one, two = (np.array(pairs) for pairs in PAIRS8[:2])
+    starts = [np.arange(NZ), two, two[one], two[one[two]]]
+    zs_a = jnp.array(np.stack([v for at in starts for v in (at, one[at])], axis=1), jnp.int32)[z]
     table = jnp.concatenate(
         [
             ((xa % 2) * NY + ya).reshape(16),
@@ -357,14 +392,15 @@
         ]
     ).astype(jnp.int32)
 
+    heads = [head.reshape(NZ, -1, COLS) for head in (head_t, head_t_other, head_r, head_r_other)]
+    early = preload(table, *heads[:2])
     wide_gain_t = gain_t.astype(jnp.float32).reshape(16, 1, WT)
     wide_gain_r = gain_r.astype(jnp.float32).reshape(16, 1, WR)
     logits, logits_cross, stats = heads_call(
         table,
         wide_gain_t, wide_gain_r,
         *blocks_a, *blocks_c,
-        head_t.reshape(NZ, 2 * WT, COLS), head_t_other.reshape(NZ, 2 * WT, COLS),
-        head_r.reshape(NZ, 2 * WR, COLS), head_r_other.reshape(NZ, 2 * WR, COLS),
+        *heads, early,
     )
 
     logits_other = send(logits_cross, other_core)

time: 156 us -> 152 us (0.974)
  waiting for transfers between devices: 51.3 us -> 41.6 us
  starting transfers between devices: 64.9 us -> 70.9 us
  other arithmetic: 9.14 us -> 7.26 us
    ppermute x34 -> x35, waiting for transfers between devices: 51.3 us -> 41.6 us  [send(): return lax.ppermute(value, AXES, pairs)]
    ppermute x34 -> x35, starting transfers between devices: 64.9 us -> 70.9 us  [send(): return lax.ppermute(value, AXES, pairs)]
    pallas_call x0 -> x1, Pallas kernels: none -> 4.28 us  [preload(): pl.pallas_call(preload_kernel, out_shape=pltpu.VMEM((EARLY, 2, 2 * WT, CO...]
    pallas_call x1, Pallas kernels: 18.3 us -> 14.7 us  [heads_call(): pl.pallas_call(heads_kernel, out_shape=[square] * 2 + [jax.ShapeDtypeStru...]
    unnamed x20 -> x24, local copies, waits for them, and re-layouts: 3.44 us -> 4.25 us
  transfers between devices with their start and end apart: 34 -> 35, of which waited for: 19 -> 20; matrix products, arithmetic and copies ran while one was open for 10% -> 9% of each run, Pallas kernels for 0% -> 3%
where the time goes in v2:
time: 152 us; the launch traced here: 151 us
  starting transfers between devices  70.9 us (47%)
  waiting for transfers between devices  41.6 us (27%)
  Pallas kernels  21.6 us (14%)
  local copies, waits for them, and re-layouts  9.62 us (6%)
  other arithmetic  7.26 us (5%)
    ppermute x35, starting transfers between devices, send(): return lax.ppermute(value, AXES, pairs)  70.9 us
    ppermute x35, waiting for transfers between devices, send(): return lax.ppermute(value, AXES, pairs)  41.6 us
    pallas_call x1, Pallas kernels, heads_call(): pl.pallas_call(heads_kernel, out_shape=[square] * 2 + [jax.ShapeDtypeStru...  14.7 us
    pallas_call x1, Pallas kernels, preload(): pl.pallas_call(preload_kernel, out_shape=pltpu.VMEM((EARLY, 2, 2 * WT, CO...  4.28 us
    unnamed x24, local copies, waits for them, and re-layouts  4.25 us
  transfers between devices with their start and end apart: 35, of which 20 were waited for; matrix products, arithmetic and copies ran while one was open for 9% of the time, Pallas kernels for 3%

profile of v2, /device:TPU:1, one launch (start us, length us, event | category | flops | bytes accessed | tf_op | source)
XLA Modules:
  0.0 151.3 jit_solution(16627758864109968189)
XLA Ops:
  0.0 3.2 %collective-permute-start.8 = (bf16[16384,256]{1,0:T(8,128)(2,1)}, bf16[16384,256]{1,0:T(8,128)(2,1)S(1)}, u32[]{:S(2)}, u32[]{:S(2)}) collective-permute-start(bf16[16384,256]{1,0:T(8,128)(2,1)} %param.15), channel_id=1, source_target_pairs={{0,16},{1,17},{2,18},{3,19},{4,20},{5,21},{6,22},{7,23},{8,24},{9,... | collective-permute-start | bytes 25165832 | tf_op jit(solution)/shard_map/ppermute | solution.py:40
  9.7 5.5 %collective-permute-start.3 = (bf16[2,32,896]{2,1,0:T(8,128)(2,1)S(1)}, bf16[2,32,896]{2,1,0:T(8,128)(2,1)S(1)}, u32[]{:S(2)}, u32[]{:S(2)}) collective-permute-start(bf16[2,32,896]{2,1,0:T(8,128)(2,1)S(1)} %pad_maximum_fusion.3), channel_id=1, source_target_pairs={{0,14},{1,15},{2,4},{3,5},{4,2},{5,3},{6,8},{7,9},{8,6},{9,7},{10,... | collective-permute-start | bytes 344072 | tf_op jit(solution)/shard_map/ppermute | solution.py:40
  22.7 3.3 %collective-permute-done.6 = bf16[2,32,896]{2,1,0:T(8,128)(2,1)S(1)} collective-permute-done((bf16[2,32,896]{2,1,0:T(8,128)(2,1)S(1)}, bf16[2,32,896]{2,1,0:T(8,128)(2,1)S(1)}, u32[]{:S(2)}, u32[]{:S(2)}) %collective-permute-start.6) | collective-permute-done | bytes 114720 | tf_op jit(solution)/shard_map/ppermute | solution.py:40
  26.4 3.5 %collective-permute-start.10 = (bf16[1,8,32,896]{3,2,1,0:T(8,128)(2,1)S(1)}, bf16[1,8,32,896]{3,2,1,0:T(8,128)(2,1)S(1)}, u32[]{:S(2)}, u32[]{:S(2)}) collective-permute-start(bf16[1,8,32,896]{3,2,1,0:T(8,128)(2,1)S(1)} %bitcast.29), channel_id=1, source_target_pairs={{0,96},{1,97},{2,98},{3,99},{4,100},{5,101},{6,102},{7,103},{8,104... | collective-permute-start | bytes 1376264 | tf_op jit(solution)/shard_map/ppermute | solution.py:40
  31.3 4.7 %collective-permute-done.9 = bf16[1,8,32,896]{3,2,1,0:T(8,128)(2,1)} collective-permute-done((bf16[1,8,32,896]{3,2,1,0:T(8,128)(2,1)S(1)}, bf16[1,8,32,896]{3,2,1,0:T(8,128)(2,1)}, u32[]{:S(2)}, u32[]{:S(2)}) %collective-permute-start.9) | collective-permute-done | bytes 458784 | tf_op jit(solution)/shard_map/ppermute | solution.py:40
  38.2 2.7 %collective-permute-start.14 = (bf16[2,8,32,896]{3,2,1,0:T(8,128)(2,1)S(1)}, bf16[2,8,32,896]{3,2,1,0:T(8,128)(2,1)}, u32[]{:S(2)}, u32[]{:S(2)}) collective-permute-start(bf16[2,8,32,896]{3,2,1,0:T(8,128)(2,1)S(1)} %pad_maximum_fusion.refs_3_), channel_id=1, source_target_pairs={{0,129},{1,128},{2,131},{3,130},{4,133},{5,132},{6,135},{7,134},{8... | collective-permute-start | bytes 2752520 | tf_op jit(solution)/shard_map/ppermute | solution.py:40
  43.3 2.7 %collective-permute-start.16 = (bf16[16,32,384]{2,1,0:T(8,128)(2,1)S(1)}, bf16[16,32,384]{2,1,0:T(8,128)(2,1)}, u32[]{:S(2)}, u32[]{:S(2)}) collective-permute-start(bf16[16,32,384]{2,1,0:T(8,128)(2,1)S(1)} %constant_dynamic-update-slice_fusion.2.refs_11_), channel_id=1, source_target_pairs={{0,14},{1,15},{2,0},{3,1},{4,2},{5,3},{6,4},{7,5},{8,6},{9,7},{10,... | collective-permute-start | bytes 1179656 | tf_op jit(solution)/shard_map/ppermute | solution.py:40
  48.5 5.2 %collective-permute-done.12 = bf16[1,8,32,896]{3,2,1,0:T(8,128)(2,1)} collective-permute-done((bf16[1,8,32,896]{3,2,1,0:T(8,128)(2,1)}, bf16[1,8,32,896]{3,2,1,0:T(8,128)(2,1)}, u32[]{:S(2)}, u32[]{:S(2)}) %collective-permute-start.12) | collective-permute-done | bytes 458784 | tf_op jit(solution)/shard_map/ppermute | solution.py:40
  55.9 2.7 %collective-permute-start.18 = (bf16[2,8,32,896]{3,2,1,0:T(8,128)(2,1)}, bf16[2,8,32,896]{3,2,1,0:T(8,128)(2,1)}, u32[]{:S(2)}, u32[]{:S(2)}) collective-permute-start(bf16[2,8,32,896]{3,2,1,0:T(8,128)(2,1)} %constant_dynamic-update-slice_fusion.refs_4_), channel_id=1, source_target_pairs={{0,129},{1,128},{2,131},{3,130},{4,133},{5,132},{6,135},{7,134},{8... | collective-permute-start | bytes 2752520 | tf_op jit(solution)/shard_map/ppermute | solution.py:40
  58.6 2.7 %collective-permute-start.22 = (bf16[16,32,384]{2,1,0:T(8,128)(2,1)}, bf16[16,32,384]{2,1,0:T(8,128)(2,1)}, u32[]{:S(2)}, u32[]{:S(2)}) collective-permute-start(bf16[16,32,384]{2,1,0:T(8,128)(2,1)} %collective-permute-done.16.refs_13_), channel_id=1, source_target_pairs={{0,14},{1,15},{2,0},{3,1},{4,2},{5,3},{6,4},{7,5},{8,6},{9,7},{10,... | collective-permute-start | bytes 1179656 | tf_op jit(solution)/shard_map/ppermute | solution.py:40
  67.1 2.7 %collective-permute-start.24 = (bf16[16,32,384]{2,1,0:T(8,128)(2,1)}, bf16[16,32,384]{2,1,0:T(8,128)(2,1)S(1)}, u32[]{:S(2)}, u32[]{:S(2)}) collective-permute-start(bf16[16,32,384]{2,1,0:T(8,128)(2,1)} %collective-permute-done.22.refs_15_), channel_id=1, source_target_pairs={{0,14},{1,15},{2,0},{3,1},{4,2},{5,3},{6,4},{7,5},{8,6},{9,7},{10,... | collective-permute-start | bytes 1179656 | tf_op jit(solution)/shard_map/ppermute | solution.py:40
  69.9 2.7 %collective-permute-start.20 = (bf16[2,8,32,896]{3,2,1,0:T(8,128)(2,1)}, bf16[2,8,32,896]{3,2,1,0:T(8,128)(2,1)}, u32[]{:S(2)}, u32[]{:S(2)}) collective-permute-start(bf16[2,8,32,896]{3,2,1,0:T(8,128)(2,1)} %collective-permute-done.18.refs_8_), channel_id=1, source_target_pairs={{0,129},{1,128},{2,131},{3,130},{4,133},{5,132},{6,135},{7,134},{8... | collective-permute-start | bytes 2752520 | tf_op jit(solution)/shard_map/ppermute | solution.py:40
  72.6 3.7 %collective-permute-done.23.refs_16_ = bf16[16,32,384]{2,1,0:T(8,128)(2,1)S(1)} collective-permute-done((bf16[16,32,384]{2,1,0:T(8,128)(2,1)}, bf16[16,32,384]{2,1,0:T(8,128)(2,1)S(1)}, u32[]{:S(2)}, u32[]{:S(2)}) %collective-permute-start.23) | collective-permute-done | bytes 393248 | tf_op jit(solution)/shard_map/ppermute | solution.py:40
  77.9 3.0 %collective-permute-start.25 = (bf16[16,32,384]{2,1,0:T(8,128)(2,1)}, bf16[16,32,384]{2,1,0:T(8,128)(2,1)}, u32[]{:S(2)}, u32[]{:S(2)}) collective-permute-start(bf16[16,32,384]{2,1,0:T(8,128)(2,1)} %broadcast_select_fusion), channel_id=1, source_target_pairs={{0,2},{1,3},{2,4},{3,5},{4,6},{5,7},{6,8},{7,9},{8,10},{9,11},{10,... | collective-permute-start | bytes 1179656 | tf_op jit(solution)/shard_map/ppermute | solution.py:40
  82.4 4.3 %preload.1.refs_23_ = bf16[4,2,2048,256]{3,2,1,0:T(8,128)(2,1)S(1)} custom-call(s32[80]{0:T(128)S(1)} %concatenate.51.table_ref.refs_0_, bf16[8,2048,256]{2,1,0:T(8,128)(2,1)} %bitcast.24, bf16[8,2048,256]{2,1,0:T(8,128)(2,1)} %bitcast.26), custom_call_target="tpu_custom_call" | custom-call | tf_op jit(solution)/shard_map/preload/pallas_call | solution.py:122
  87.6 14.7 %heads.1 = (f32[2,256,256]{2,1,0:T(8,128)S(1)}, f32[2,256,256]{2,1,0:T(8,128)S(1)}, f32[8,256]{1,0:T(8,128)S(1)}) custom-call(s32[80]{0:T(128)S(1)} %concatenate.51.table_ref.refs_0_, f32[16,1,1024]{2,1,0:T(1,128)S(1)} %bitcast.22, f32[16,1,256]{2,1,0:T(1,128)S(1)} %bitcast.23, bf16[2,8,32,896]{3,2,1,0:T(8,128)(2,1)S(1)} %pad_maximum_fusion.refs_3_, ...), custom_call_target="tpu_custom_call" | custom-call | tf_op jit(solution)/shard_map/heads/pallas_call | solution.py:306
  103.1 2.9 %collective-permute-start.26 = (f32[8,256]{1,0:T(8,128)S(1)}, f32[8,256]{1,0:T(8,128)S(1)}, u32[]{:S(2)}, u32[]{:S(2)}) collective-permute-start(f32[8,256]{1,0:T(8,128)S(1)} %get-tuple-element.34), channel_id=1, source_target_pairs={{0,128},{1,129},{2,130},{3,131},{4,132},{5,133},{6,134},{7,135},{8... | collective-permute-start | bytes 24584 | tf_op jit(solution)/shard_map/ppermute | solution.py:40
  107.7 3.3 %collective-permute-done.27 = f32[8,256]{1,0:T(8,128)S(1)} collective-permute-done((f32[8,256]{1,0:T(8,128)S(1)}, f32[8,256]{1,0:T(8,128)S(1)}, u32[]{:S(2)}, u32[]{:S(2)}) %collective-permute-start.27) | collective-permute-done | bytes 8224 | tf_op jit(solution)/shard_map/ppermute | solution.py:40
  114.7 2.7 %collective-permute-done.29 = f32[8,256]{1,0:T(8,128)S(1)} collective-permute-done((f32[8,256]{1,0:T(8,128)S(1)}, f32[8,256]{1,0:T(8,128)S(1)}, u32[]{:S(2)}, u32[]{:S(2)}) %collective-permute-start.29) | collective-permute-done | bytes 8224 | tf_op jit(solution)/shard_map/ppermute | solution.py:40
  117.5 2.8 %collective-permute-done.30 = f32[8,256]{1,0:T(8,128)S(1)} collective-permute-done((f32[8,256]{1,0:T(8,128)S(1)}, f32[8,256]{1,0:T(8,128)S(1)}, u32[]{:S(2)}, u32[]{:S(2)}) %collective-permute-start.30) | collective-permute-done | bytes 8224 | tf_op jit(solution)/shard_map/ppermute | solution.py:40
  120.4 3.1 %collective-permute-start.31 = (f32[8,256]{1,0:T(8,128)S(1)}, f32[8,256]{1,0:T(8,128)S(1)}, u32[]{:S(2)}, u32[]{:S(2)}) collective-permute-start(f32[8,256]{1,0:T(8,128)S(1)} %maximum_maximum_fusion.4), channel_id=1, source_target_pairs={{0,14},{1,15},{2,4},{3,5},{4,2},{5,3},{6,8},{7,9},{8,6},{9,7},{10,... | collective-permute-start | bytes 24584 | tf_op jit(solution)/shard_map/ppermute | solution.py:40
  123.5 15.0 %collective-permute-start.34 = (f32[2,256,256]{2,1,0:T(8,128)S(1)}, f32[2,256,256]{2,1,0:T(8,128)S(1)}, u32[]{:S(2)}, u32[]{:S(2)}) collective-permute-start(f32[2,256,256]{2,1,0:T(8,128)S(1)} %get-tuple-element.36), channel_id=1, source_target_pairs={{0,16},{1,17},{2,18},{3,19},{4,20},{5,21},{6,22},{7,23},{8,24},{9,... | collective-permute-start | bytes 1572872 | tf_op jit(solution)/shard_map/ppermute | solution.py:40
  139.8 3.0 %collective-permute-done.32 = f32[8,256]{1,0:T(8,128)S(1)} collective-permute-done((f32[8,256]{1,0:T(8,128)S(1)}, f32[8,256]{1,0:T(8,128)S(1)}, u32[]{:S(2)}, u32[]{:S(2)}) %collective-permute-start.32) | collective-permute-done | bytes 8224 | tf_op jit(solution)/shard_map/ppermute | solution.py:40
  143.0 4.0 %collective-permute-start.33 = (f32[8,256]{1,0:T(8,128)S(1)}, f32[8,256]{1,0:T(8,128)S(1)}, u32[]{:S(2)}, u32[]{:S(2)}) collective-permute-start(f32[8,256]{1,0:T(8,128)S(1)} %maximum_maximum_fusion.6.own_ref), channel_id=1, source_target_pairs={{0,16},{1,17},{2,18},{3,19},{4,20},{5,21},{6,22},{7,23},{8,24},{9,... | collective-permute-start | bytes 24584 | tf_op jit(solution)/shard_map/ppermute | solution.py:40
  (118 shorter events, 47.0 us)
Async XLA Ops:
  0.0 26.0 %collective-permute-start.8 = (bf16[16384,256]{1,0:T(8,128)(2,1)}, bf16[16384,256]{1,0:T(8,128)(2,1)S(1)}, u32[]{:S(2)}, u32[]{:S(2)}) collective-permute-start(bf16[16384,256]{1,0:T(8,128)(2,1)} %param.15), channel_id=1, source_target_pairs={{0,16},{1,17},{2,18},{3,19},{4,20},{5,21},{6,22},{7,23},{8,24},{9,... | collective-permute-start | bytes 25165832 | tf_op jit(solution)/shard_map/ppermute | solution.py:40
  3.2 22.8 %collective-permute-start.7 = (bf16[4096,256]{1,0:T(8,128)(2,1)}, bf16[4096,256]{1,0:T(8,128)(2,1)S(1)}, u32[]{:S(2)}, u32[]{:S(2)}) collective-permute-start(bf16[4096,256]{1,0:T(8,128)(2,1)} %param.18), channel_id=1, source_target_pairs={{0,16},{1,17},{2,18},{3,19},{4,20},{5,21},{6,22},{7,23},{8,24},{9,... | collective-permute-start | bytes 6291464 | tf_op jit(solution)/shard_map/ppermute | solution.py:40
  8.0 7.3 %collective-permute-start.2 = (bf16[2,32,384]{2,1,0:T(8,128)(2,1)S(1)}, bf16[2,32,384]{2,1,0:T(8,128)(2,1)S(1)}, u32[]{:S(2)}, u32[]{:S(2)}) collective-permute-start(bf16[2,32,384]{2,1,0:T(8,128)(2,1)S(1)} %pad_maximum_fusion.5), channel_id=1, source_target_pairs={{0,129},{1,128},{2,131},{3,130},{4,133},{5,132},{6,135},{7,134},{8... | collective-permute-start | bytes 147464 | tf_op jit(solution)/shard_map/ppermute | solution.py:40
  9.7 7.7 %collective-permute-start.3 = (bf16[2,32,896]{2,1,0:T(8,128)(2,1)S(1)}, bf16[2,32,896]{2,1,0:T(8,128)(2,1)S(1)}, u32[]{:S(2)}, u32[]{:S(2)}) collective-permute-start(bf16[2,32,896]{2,1,0:T(8,128)(2,1)S(1)} %pad_maximum_fusion.3), channel_id=1, source_target_pairs={{0,14},{1,15},{2,4},{3,5},{4,2},{5,3},{6,8},{7,9},{8,6},{9,7},{10,... | collective-permute-start | bytes 344072 | tf_op jit(solution)/shard_map/ppermute | solution.py:40
  19.0 6.9 %collective-permute-start.6 = (bf16[2,32,896]{2,1,0:T(8,128)(2,1)S(1)}, bf16[2,32,896]{2,1,0:T(8,128)(2,1)S(1)}, u32[]{:S(2)}, u32[]{:S(2)}) collective-permute-start(bf16[2,32,896]{2,1,0:T(8,128)(2,1)S(1)} %collective-permute-done.3), channel_id=1, source_target_pairs={{0,4},{1,5},{2,14},{3,15},{4,8},{5,9},{6,2},{7,3},{8,12},{9,13},{1... | collective-permute-start | bytes 344072 | tf_op jit(solution)/shard_map/ppermute | solution.py:40
  26.1 10.0 %collective-permute-start.9 = (bf16[1,8,32,896]{3,2,1,0:T(8,128)(2,1)S(1)}, bf16[1,8,32,896]{3,2,1,0:T(8,128)(2,1)}, u32[]{:S(2)}, u32[]{:S(2)}) collective-permute-start(bf16[1,8,32,896]{3,2,1,0:T(8,128)(2,1)S(1)} %bitcast.28), channel_id=1, source_target_pairs={{0,32},{1,33},{2,34},{3,35},{4,36},{5,37},{6,38},{7,39},{8,40},{9,... | collective-permute-start | bytes 1376264 | tf_op jit(solution)/shard_map/ppermute | solution.py:40
  26.4 11.8 %collective-permute-start.10 = (bf16[1,8,32,896]{3,2,1,0:T(8,128)(2,1)S(1)}, bf16[1,8,32,896]{3,2,1,0:T(8,128)(2,1)S(1)}, u32[]{:S(2)}, u32[]{:S(2)}) collective-permute-start(bf16[1,8,32,896]{3,2,1,0:T(8,128)(2,1)S(1)} %bitcast.29), channel_id=1, source_target_pairs={{0,96},{1,97},{2,98},{3,99},{4,100},{5,101},{6,102},{7,103},{8,104... | collective-permute-start | bytes 1376264 | tf_op jit(solution)/shard_map/ppermute | solution.py:40
  29.9 8.3 %collective-permute-start.11 = (bf16[8,32,384]{2,1,0:T(8,128)(2,1)S(1)}, bf16[8,32,384]{2,1,0:T(8,128)(2,1)S(1)}, u32[]{:S(2)}, u32[]{:S(2)}) collective-permute-start(bf16[8,32,384]{2,1,0:T(8,128)(2,1)S(1)} %pad_maximum_fusion.2), channel_id=1, source_target_pairs={{0,96},{1,97},{2,98},{3,99},{4,100},{5,101},{6,102},{7,103},{8,104... | collective-permute-start | bytes 589832 | tf_op jit(solution)/shard_map/ppermute | solution.py:40
  38.2 17.4 %collective-permute-start.13 = (bf16[2,8,32,896]{3,2,1,0:T(8,128)(2,1)S(1)}, bf16[2,8,32,896]{3,2,1,0:T(8,128)(2,1)}, u32[]{:S(2)}, u32[]{:S(2)}) collective-permute-start(bf16[2,8,32,896]{3,2,1,0:T(8,128)(2,1)S(1)} %pad_maximum_fusion.refs_3_), channel_id=1, source_target_pairs={{0,128},{1,129},{2,130},{3,131},{4,132},{5,133},{6,134},{7,135},{8... | collective-permute-start | bytes 2752520 | tf_op jit(solution)/shard_map/ppermute | solution.py:40
  38.2 17.4 %collective-permute-start.14 = (bf16[2,8,32,896]{3,2,1,0:T(8,128)(2,1)S(1)}, bf16[2,8,32,896]{3,2,1,0:T(8,128)(2,1)}, u32[]{:S(2)}, u32[]{:S(2)}) collective-permute-start(bf16[2,8,32,896]{3,2,1,0:T(8,128)(2,1)S(1)} %pad_maximum_fusion.refs_3_), channel_id=1, source_target_pairs={{0,129},{1,128},{2,131},{3,130},{4,133},{5,132},{6,135},{7,134},{8... | collective-permute-start | bytes 2752520 | tf_op jit(solution)/shard_map/ppermute | solution.py:40
  40.8 12.9 %collective-permute-start.12 = (bf16[1,8,32,896]{3,2,1,0:T(8,128)(2,1)}, bf16[1,8,32,896]{3,2,1,0:T(8,128)(2,1)}, u32[]{:S(2)}, u32[]{:S(2)}) collective-permute-start(bf16[1,8,32,896]{3,2,1,0:T(8,128)(2,1)} %collective-permute-done.9), channel_id=1, source_target_pairs={{0,32},{1,33},{2,34},{3,35},{4,36},{5,37},{6,38},{7,39},{8,40},{9,... | collective-permute-start | bytes 1376264 | tf_op jit(solution)/shard_map/ppermute | solution.py:40
  43.2 12.4 %collective-permute-start.15 = (bf16[16,32,384]{2,1,0:T(8,128)(2,1)S(1)}, bf16[16,32,384]{2,1,0:T(8,128)(2,1)}, u32[]{:S(2)}, u32[]{:S(2)}) collective-permute-start(bf16[16,32,384]{2,1,0:T(8,128)(2,1)S(1)} %constant_dynamic-update-slice_fusion.2.refs_11_), channel_id=1, source_target_pairs={{0,2},{1,3},{2,4},{3,5},{4,6},{5,7},{6,8},{7,9},{8,10},{9,11},{10,... | collective-permute-start | bytes 1179656 | tf_op jit(solution)/shard_map/ppermute | solution.py:40
  43.3 12.3 %collective-permute-start.16 = (bf16[16,32,384]{2,1,0:T(8,128)(2,1)S(1)}, bf16[16,32,384]{2,1,0:T(8,128)(2,1)}, u32[]{:S(2)}, u32[]{:S(2)}) collective-permute-start(bf16[16,32,384]{2,1,0:T(8,128)(2,1)S(1)} %constant_dynamic-update-slice_fusion.2.refs_11_), channel_id=1, source_target_pairs={{0,14},{1,15},{2,0},{3,1},{4,2},{5,3},{6,4},{7,5},{8,6},{9,7},{10,... | collective-permute-start | bytes 1179656 | tf_op jit(solution)/shard_map/ppermute | solution.py:40
  55.6 14.3 %collective-permute-start.17 = (bf16[2,8,32,896]{3,2,1,0:T(8,128)(2,1)}, bf16[2,8,32,896]{3,2,1,0:T(8,128)(2,1)}, u32[]{:S(2)}, u32[]{:S(2)}) collective-permute-start(bf16[2,8,32,896]{3,2,1,0:T(8,128)(2,1)} %constant_dynamic-update-slice_fusion.refs_4_), channel_id=1, source_target_pairs={{0,128},{1,129},{2,130},{3,131},{4,132},{5,133},{6,134},{7,135},{8... | collective-permute-start | bytes 2752520 | tf_op jit(solution)/shard_map/ppermute | solution.py:40
  55.9 14.1 %collective-permute-start.18 = (bf16[2,8,32,896]{3,2,1,0:T(8,128)(2,1)}, bf16[2,8,32,896]{3,2,1,0:T(8,128)(2,1)}, u32[]{:S(2)}, u32[]{:S(2)}) collective-permute-start(bf16[2,8,32,896]{3,2,1,0:T(8,128)(2,1)} %constant_dynamic-update-slice_fusion.refs_4_), channel_id=1, source_target_pairs={{0,129},{1,128},{2,131},{3,130},{4,133},{5,132},{6,135},{7,134},{8... | collective-permute-start | bytes 2752520 | tf_op jit(solution)/shard_map/ppermute | solution.py:40
  58.6 8.4 %collective-permute-start.21 = (bf16[16,32,384]{2,1,0:T(8,128)(2,1)}, bf16[16,32,384]{2,1,0:T(8,128)(2,1)}, u32[]{:S(2)}, u32[]{:S(2)}) collective-permute-start(bf16[16,32,384]{2,1,0:T(8,128)(2,1)} %collective-permute-done.15.refs_12_), channel_id=1, source_target_pairs={{0,2},{1,3},{2,4},{3,5},{4,6},{5,7},{6,8},{7,9},{8,10},{9,11},{10,... | collective-permute-start | bytes 1179656 | tf_op jit(solution)/shard_map/ppermute | solution.py:40
  58.6 8.5 %collective-permute-start.22 = (bf16[16,32,384]{2,1,0:T(8,128)(2,1)}, bf16[16,32,384]{2,1,0:T(8,128)(2,1)}, u32[]{:S(2)}, u32[]{:S(2)}) collective-permute-start(bf16[16,32,384]{2,1,0:T(8,128)(2,1)} %collective-permute-done.16.refs_13_), channel_id=1, source_target_pairs={{0,14},{1,15},{2,0},{3,1},{4,2},{5,3},{6,4},{7,5},{8,6},{9,7},{10,... | collective-permute-start | bytes 1179656 | tf_op jit(solution)/shard_map/ppermute | solution.py:40
  67.1 9.3 %collective-permute-start.23 = (bf16[16,32,384]{2,1,0:T(8,128)(2,1)}, bf16[16,32,384]{2,1,0:T(8,128)(2,1)S(1)}, u32[]{:S(2)}, u32[]{:S(2)}) collective-permute-start(bf16[16,32,384]{2,1,0:T(8,128)(2,1)} %collective-permute-done.21.refs_14_), channel_id=1, source_target_pairs={{0,2},{1,3},{2,4},{3,5},{4,6},{5,7},{6,8},{7,9},{8,10},{9,11},{10,... | collective-permute-start | bytes 1179656 | tf_op jit(solution)/shard_map/ppermute | solution.py:40
  67.1 9.3 %collective-permute-start.24 = (bf16[16,32,384]{2,1,0:T(8,128)(2,1)}, bf16[16,32,384]{2,1,0:T(8,128)(2,1)S(1)}, u32[]{:S(2)}, u32[]{:S(2)}) collective-permute-start(bf16[16,32,384]{2,1,0:T(8,128)(2,1)} %collective-permute-done.22.refs_15_), channel_id=1, source_target_pairs={{0,14},{1,15},{2,0},{3,1},{4,2},{5,3},{6,4},{7,5},{8,6},{9,7},{10,... | collective-permute-start | bytes 1179656 | tf_op jit(solution)/shard_map/ppermute | solution.py:40
  69.9 17.6 %collective-permute-start.20 = (bf16[2,8,32,896]{3,2,1,0:T(8,128)(2,1)}, bf16[2,8,32,896]{3,2,1,0:T(8,128)(2,1)}, u32[]{:S(2)}, u32[]{:S(2)}) collective-permute-start(bf16[2,8,32,896]{3,2,1,0:T(8,128)(2,1)} %collective-permute-done.18.refs_8_), channel_id=1, source_target_pairs={{0,129},{1,128},{2,131},{3,130},{4,133},{5,132},{6,135},{7,134},{8... | collective-permute-start | bytes 2752520 | tf_op jit(solution)/shard_map/ppermute | solution.py:40
  72.6 15.0 %collective-permute-start.19 = (bf16[2,8,32,896]{3,2,1,0:T(8,128)(2,1)}, bf16[2,8,32,896]{3,2,1,0:T(8,128)(2,1)}, u32[]{:S(2)}, u32[]{:S(2)}) collective-permute-start(bf16[2,8,32,896]{3,2,1,0:T(8,128)(2,1)} %collective-permute-done.13.refs_5_), channel_id=1, source_target_pairs={{0,128},{1,129},{2,130},{3,131},{4,132},{5,133},{6,134},{7,135},{8... | collective-permute-start | bytes 2752520 | tf_op jit(solution)/shard_map/ppermute | solution.py:40
  77.9 9.6 %collective-permute-start.25 = (bf16[16,32,384]{2,1,0:T(8,128)(2,1)}, bf16[16,32,384]{2,1,0:T(8,128)(2,1)}, u32[]{:S(2)}, u32[]{:S(2)}) collective-permute-start(bf16[16,32,384]{2,1,0:T(8,128)(2,1)} %broadcast_select_fusion), channel_id=1, source_target_pairs={{0,2},{1,3},{2,4},{3,5},{4,6},{5,7},{6,8},{7,9},{8,10},{9,11},{10,... | collective-permute-start | bytes 1179656 | tf_op jit(solution)/shard_map/ppermute | solution.py:40
  120.4 18.1 %collective-permute-start.31 = (f32[8,256]{1,0:T(8,128)S(1)}, f32[8,256]{1,0:T(8,128)S(1)}, u32[]{:S(2)}, u32[]{:S(2)}) collective-permute-start(f32[8,256]{1,0:T(8,128)S(1)} %maximum_maximum_fusion.4), channel_id=1, source_target_pairs={{0,14},{1,15},{2,4},{3,5},{4,2},{5,3},{6,8},{7,9},{8,6},{9,7},{10,... | collective-permute-start | bytes 24584 | tf_op jit(solution)/shard_map/ppermute | solution.py:40
  123.5 24.4 %collective-permute-start.34 = (f32[2,256,256]{2,1,0:T(8,128)S(1)}, f32[2,256,256]{2,1,0:T(8,128)S(1)}, u32[]{:S(2)}, u32[]{:S(2)}) collective-permute-start(f32[2,256,256]{2,1,0:T(8,128)S(1)} %get-tuple-element.36), channel_id=1, source_target_pairs={{0,16},{1,17},{2,18},{3,19},{4,20},{5,21},{6,22},{7,23},{8,24},{9,... | collective-permute-start | bytes 1572872 | tf_op jit(solution)/shard_map/ppermute | solution.py:40
  (22 other events, 94.4 us)

commit v3 on v2

--- a/solution.py
+++ b/solution.py
@@ -414,8 +414,15 @@
         out_shape=jax.ShapeDtypeStruct((8, 2, GROUP, COLS), jnp.float32),
         in_specs=[smem] + [vmem] * 4,
         out_specs=vmem,
+        compiler_params=pltpu.CompilerParams(vmem_limit_bytes=8 * 2**20),
         name="contrast",
-    )(core.astype(jnp.int32).reshape(1), stats, stats_other, logits, logits_other)
+    )(
+        core.astype(jnp.int32).reshape(1),
+        *(
+            pltpu.with_memory_space_constraint(value, pltpu.VMEM)
+            for value in (stats, stats_other, logits, logits_other)
+        ),
+    )
     return out.reshape(2 * ROWS, COLS)
 
 

time: 152 us -> 149 us (0.980)
  local copies, waits for them, and re-layouts: 9.62 us -> 8 us
    unnamed x24 -> x16, local copies, waits for them, and re-layouts: 4.25 us -> 2.63 us
where the time goes in v3:
time: 149 us
  starting transfers between devices  71.4 us (48%)
  waiting for transfers between devices  41.5 us (28%)
  Pallas kernels  20.4 us (14%)
  local copies, waits for them, and re-layouts  8 us (5%)
  other arithmetic  7.22 us (5%)
    ppermute x35, starting transfers between devices, send(): return lax.ppermute(value, AXES, pairs)  71.4 us
    ppermute x35, waiting for transfers between devices, send(): return lax.ppermute(value, AXES, pairs)  41.5 us
    pallas_call x1, Pallas kernels, heads_call(): pl.pallas_call(heads_kernel, out_shape=[square] * 2 + [jax.ShapeDtypeStru...  14.7 us
    pallas_call x1, Pallas kernels, preload(): pl.pallas_call(preload_kernel, out_shape=pltpu.VMEM((EARLY, 2, 2 * WT, CO...  4.28 us
  transfers between devices with their start and end apart: 35, of which 20 were waited for; matrix products, arithmetic and copies ran while one was open for 9% of the time, Pallas kernels for 3%

profile of v3, /device:TPU:1, one launch (start us, length us, event | category | flops | bytes accessed | tf_op | source)
XLA Modules:
  0.0 148.7 jit_solution(11218898757260762461)
XLA Ops:
  0.0 3.2 %collective-permute-start.8 = (bf16[16384,256]{1,0:T(8,128)(2,1)}, bf16[16384,256]{1,0:T(8,128)(2,1)S(1)}, u32[]{:S(2)}, u32[]{:S(2)}) collective-permute-start(bf16[16384,256]{1,0:T(8,128)(2,1)} %param.15), channel_id=1, source_target_pairs={{0,16},{1,17},{2,18},{3,19},{4,20},{5,21},{6,22},{7,23},{8,24},{9,... | collective-permute-start | bytes 25165832 | tf_op jit(solution)/shard_map/ppermute | solution.py:40
  9.7 5.5 %collective-permute-start.3 = (bf16[2,32,896]{2,1,0:T(8,128)(2,1)S(1)}, bf16[2,32,896]{2,1,0:T(8,128)(2,1)S(1)}, u32[]{:S(2)}, u32[]{:S(2)}) collective-permute-start(bf16[2,32,896]{2,1,0:T(8,128)(2,1)S(1)} %pad_maximum_fusion.3), channel_id=1, source_target_pairs={{0,14},{1,15},{2,4},{3,5},{4,2},{5,3},{6,8},{7,9},{8,6},{9,7},{10,... | collective-permute-start | bytes 344072 | tf_op jit(solution)/shard_map/ppermute | solution.py:40
  22.7 3.3 %collective-permute-done.6 = bf16[2,32,896]{2,1,0:T(8,128)(2,1)S(1)} collective-permute-done((bf16[2,32,896]{2,1,0:T(8,128)(2,1)S(1)}, bf16[2,32,896]{2,1,0:T(8,128)(2,1)S(1)}, u32[]{:S(2)}, u32[]{:S(2)}) %collective-permute-start.6) | collective-permute-done | bytes 114720 | tf_op jit(solution)/shard_map/ppermute | solution.py:40
  26.4 3.5 %collective-permute-start.10 = (bf16[1,8,32,896]{3,2,1,0:T(8,128)(2,1)S(1)}, bf16[1,8,32,896]{3,2,1,0:T(8,128)(2,1)S(1)}, u32[]{:S(2)}, u32[]{:S(2)}) collective-permute-start(bf16[1,8,32,896]{3,2,1,0:T(8,128)(2,1)S(1)} %bitcast.29), channel_id=1, source_target_pairs={{0,96},{1,97},{2,98},{3,99},{4,100},{5,101},{6,102},{7,103},{8,104... | collective-permute-start | bytes 1376264 | tf_op jit(solution)/shard_map/ppermute | solution.py:40
  31.3 4.7 %collective-permute-done.9 = bf16[1,8,32,896]{3,2,1,0:T(8,128)(2,1)} collective-permute-done((bf16[1,8,32,896]{3,2,1,0:T(8,128)(2,1)S(1)}, bf16[1,8,32,896]{3,2,1,0:T(8,128)(2,1)}, u32[]{:S(2)}, u32[]{:S(2)}) %collective-permute-start.9) | collective-permute-done | bytes 458784 | tf_op jit(solution)/shard_map/ppermute | solution.py:40
  38.2 2.7 %collective-permute-start.14 = (bf16[2,8,32,896]{3,2,1,0:T(8,128)(2,1)S(1)}, bf16[2,8,32,896]{3,2,1,0:T(8,128)(2,1)}, u32[]{:S(2)}, u32[]{:S(2)}) collective-permute-start(bf16[2,8,32,896]{3,2,1,0:T(8,128)(2,1)S(1)} %pad_maximum_fusion.refs_3_), channel_id=1, source_target_pairs={{0,129},{1,128},{2,131},{3,130},{4,133},{5,132},{6,135},{7,134},{8... | collective-permute-start | bytes 2752520 | tf_op jit(solution)/shard_map/ppermute | solution.py:40
  43.3 2.7 %collective-permute-start.16 = (bf16[16,32,384]{2,1,0:T(8,128)(2,1)S(1)}, bf16[16,32,384]{2,1,0:T(8,128)(2,1)}, u32[]{:S(2)}, u32[]{:S(2)}) collective-permute-start(bf16[16,32,384]{2,1,0:T(8,128)(2,1)S(1)} %constant_dynamic-update-slice_fusion.2.refs_11_), channel_id=1, source_target_pairs={{0,14},{1,15},{2,0},{3,1},{4,2},{5,3},{6,4},{7,5},{8,6},{9,7},{10,... | collective-permute-start | bytes 1179656 | tf_op jit(solution)/shard_map/ppermute | solution.py:40
  48.5 5.2 %collective-permute-done.12 = bf16[1,8,32,896]{3,2,1,0:T(8,128)(2,1)} collective-permute-done((bf16[1,8,32,896]{3,2,1,0:T(8,128)(2,1)}, bf16[1,8,32,896]{3,2,1,0:T(8,128)(2,1)}, u32[]{:S(2)}, u32[]{:S(2)}) %collective-permute-start.12) | collective-permute-done | bytes 458784 | tf_op jit(solution)/shard_map/ppermute | solution.py:40
  55.9 2.7 %collective-permute-start.18 = (bf16[2,8,32,896]{3,2,1,0:T(8,128)(2,1)}, bf16[2,8,32,896]{3,2,1,0:T(8,128)(2,1)}, u32[]{:S(2)}, u32[]{:S(2)}) collective-permute-start(bf16[2,8,32,896]{3,2,1,0:T(8,128)(2,1)} %constant_dynamic-update-slice_fusion.refs_4_), channel_id=1, source_target_pairs={{0,129},{1,128},{2,131},{3,130},{4,133},{5,132},{6,135},{7,134},{8... | collective-permute-start | bytes 2752520 | tf_op jit(solution)/shard_map/ppermute | solution.py:40
  58.6 2.7 %collective-permute-start.22 = (bf16[16,32,384]{2,1,0:T(8,128)(2,1)}, bf16[16,32,384]{2,1,0:T(8,128)(2,1)}, u32[]{:S(2)}, u32[]{:S(2)}) collective-permute-start(bf16[16,32,384]{2,1,0:T(8,128)(2,1)} %collective-permute-done.16.refs_13_), channel_id=1, source_target_pairs={{0,14},{1,15},{2,0},{3,1},{4,2},{5,3},{6,4},{7,5},{8,6},{9,7},{10,... | collective-permute-start | bytes 1179656 | tf_op jit(solution)/shard_map/ppermute | solution.py:40
  67.1 2.7 %collective-permute-start.24 = (bf16[16,32,384]{2,1,0:T(8,128)(2,1)}, bf16[16,32,384]{2,1,0:T(8,128)(2,1)S(1)}, u32[]{:S(2)}, u32[]{:S(2)}) collective-permute-start(bf16[16,32,384]{2,1,0:T(8,128)(2,1)} %collective-permute-done.22.refs_15_), channel_id=1, source_target_pairs={{0,14},{1,15},{2,0},{3,1},{4,2},{5,3},{6,4},{7,5},{8,6},{9,7},{10,... | collective-permute-start | bytes 1179656 | tf_op jit(solution)/shard_map/ppermute | solution.py:40
  69.9 2.7 %collective-permute-start.20 = (bf16[2,8,32,896]{3,2,1,0:T(8,128)(2,1)}, bf16[2,8,32,896]{3,2,1,0:T(8,128)(2,1)}, u32[]{:S(2)}, u32[]{:S(2)}) collective-permute-start(bf16[2,8,32,896]{3,2,1,0:T(8,128)(2,1)} %collective-permute-done.18.refs_8_), channel_id=1, source_target_pairs={{0,129},{1,128},{2,131},{3,130},{4,133},{5,132},{6,135},{7,134},{8... | collective-permute-start | bytes 2752520 | tf_op jit(solution)/shard_map/ppermute | solution.py:40
  72.6 3.7 %collective-permute-done.23.refs_16_ = bf16[16,32,384]{2,1,0:T(8,128)(2,1)S(1)} collective-permute-done((bf16[16,32,384]{2,1,0:T(8,128)(2,1)}, bf16[16,32,384]{2,1,0:T(8,128)(2,1)S(1)}, u32[]{:S(2)}, u32[]{:S(2)}) %collective-permute-start.23) | collective-permute-done | bytes 393248 | tf_op jit(solution)/shard_map/ppermute | solution.py:40
  77.9 3.0 %collective-permute-start.25 = (bf16[16,32,384]{2,1,0:T(8,128)(2,1)}, bf16[16,32,384]{2,1,0:T(8,128)(2,1)}, u32[]{:S(2)}, u32[]{:S(2)}) collective-permute-start(bf16[16,32,384]{2,1,0:T(8,128)(2,1)} %broadcast_select_fusion), channel_id=1, source_target_pairs={{0,2},{1,3},{2,4},{3,5},{4,6},{5,7},{6,8},{7,9},{8,10},{9,11},{10,... | collective-permute-start | bytes 1179656 | tf_op jit(solution)/shard_map/ppermute | solution.py:40
  82.4 4.3 %preload.1.refs_23_ = bf16[4,2,2048,256]{3,2,1,0:T(8,128)(2,1)S(1)} custom-call(s32[80]{0:T(128)S(1)} %concatenate.51.table_ref.refs_0_, bf16[8,2048,256]{2,1,0:T(8,128)(2,1)} %bitcast.24, bf16[8,2048,256]{2,1,0:T(8,128)(2,1)} %bitcast.26), custom_call_target="tpu_custom_call" | custom-call | tf_op jit(solution)/shard_map/preload/pallas_call | solution.py:122
  87.6 14.7 %heads.1 = (f32[2,256,256]{2,1,0:T(8,128)S(1)}, f32[2,256,256]{2,1,0:T(8,128)S(1)}, f32[8,256]{1,0:T(8,128)S(1)}) custom-call(s32[80]{0:T(128)S(1)} %concatenate.51.table_ref.refs_0_, f32[16,1,1024]{2,1,0:T(1,128)S(1)} %bitcast.22, f32[16,1,256]{2,1,0:T(1,128)S(1)} %bitcast.23, bf16[2,8,32,896]{3,2,1,0:T(8,128)(2,1)S(1)} %pad_maximum_fusion.refs_3_, ...), custom_call_target="tpu_custom_call" | custom-call | tf_op jit(solution)/shard_map/heads/pallas_call | solution.py:306
  102.3 3.2 %collective-permute-start.26 = (f32[8,256]{1,0:T(8,128)S(1)}, f32[8,256]{1,0:T(8,128)S(1)}, u32[]{:S(2)}, u32[]{:S(2)}) collective-permute-start(f32[8,256]{1,0:T(8,128)S(1)} %get-tuple-element.34), channel_id=1, source_target_pairs={{0,128},{1,129},{2,130},{3,131},{4,132},{5,133},{6,134},{7,135},{8... | collective-permute-start | bytes 24584 | tf_op jit(solution)/shard_map/ppermute | solution.py:40
  107.2 3.2 %collective-permute-done.27 = f32[8,256]{1,0:T(8,128)S(1)} collective-permute-done((f32[8,256]{1,0:T(8,128)S(1)}, f32[8,256]{1,0:T(8,128)S(1)}, u32[]{:S(2)}, u32[]{:S(2)}) %collective-permute-start.27) | collective-permute-done | bytes 8224 | tf_op jit(solution)/shard_map/ppermute | solution.py:40
  114.2 2.7 %collective-permute-done.29 = f32[8,256]{1,0:T(8,128)S(1)} collective-permute-done((f32[8,256]{1,0:T(8,128)S(1)}, f32[8,256]{1,0:T(8,128)S(1)}, u32[]{:S(2)}, u32[]{:S(2)}) %collective-permute-start.29) | collective-permute-done | bytes 8224 | tf_op jit(solution)/shard_map/ppermute | solution.py:40
  117.0 2.8 %collective-permute-done.30 = f32[8,256]{1,0:T(8,128)S(1)} collective-permute-done((f32[8,256]{1,0:T(8,128)S(1)}, f32[8,256]{1,0:T(8,128)S(1)}, u32[]{:S(2)}, u32[]{:S(2)}) %collective-permute-start.30) | collective-permute-done | bytes 8224 | tf_op jit(solution)/shard_map/ppermute | solution.py:40
  119.8 3.1 %collective-permute-start.31 = (f32[8,256]{1,0:T(8,128)S(1)}, f32[8,256]{1,0:T(8,128)S(1)}, u32[]{:S(2)}, u32[]{:S(2)}) collective-permute-start(f32[8,256]{1,0:T(8,128)S(1)} %maximum_maximum_fusion.4), channel_id=1, source_target_pairs={{0,14},{1,15},{2,4},{3,5},{4,2},{5,3},{6,8},{7,9},{8,6},{9,7},{10,... | collective-permute-start | bytes 24584 | tf_op jit(solution)/shard_map/ppermute | solution.py:40
  123.0 15.0 %collective-permute-start.34 = (f32[2,256,256]{2,1,0:T(8,128)S(1)}, f32[2,256,256]{2,1,0:T(8,128)S(1)}, u32[]{:S(2)}, u32[]{:S(2)}) collective-permute-start(f32[2,256,256]{2,1,0:T(8,128)S(1)} %get-tuple-element.36), channel_id=1, source_target_pairs={{0,16},{1,17},{2,18},{3,19},{4,20},{5,21},{6,22},{7,23},{8,24},{9,... | collective-permute-start | bytes 1572872 | tf_op jit(solution)/shard_map/ppermute | solution.py:40
  139.3 3.1 %collective-permute-done.32 = f32[8,256]{1,0:T(8,128)S(1)} collective-permute-done((f32[8,256]{1,0:T(8,128)S(1)}, f32[8,256]{1,0:T(8,128)S(1)}, u32[]{:S(2)}, u32[]{:S(2)}) %collective-permute-start.32) | collective-permute-done | bytes 8224 | tf_op jit(solution)/shard_map/ppermute | solution.py:40
  142.5 4.0 %collective-permute-start.33 = (f32[8,256]{1,0:T(8,128)S(1)}, f32[8,256]{1,0:T(8,128)S(1)}, u32[]{:S(2)}, u32[]{:S(2)}) collective-permute-start(f32[8,256]{1,0:T(8,128)S(1)} %maximum_maximum_fusion.6.own_ref), channel_id=1, source_target_pairs={{0,16},{1,17},{2,18},{3,19},{4,20},{5,21},{6,22},{7,23},{8,24},{9,... | collective-permute-start | bytes 24584 | tf_op jit(solution)/shard_map/ppermute | solution.py:40
  (110 shorter events, 44.2 us)
Async XLA Ops:
  0.0 26.0 %collective-permute-start.8 = (bf16[16384,256]{1,0:T(8,128)(2,1)}, bf16[16384,256]{1,0:T(8,128)(2,1)S(1)}, u32[]{:S(2)}, u32[]{:S(2)}) collective-permute-start(bf16[16384,256]{1,0:T(8,128)(2,1)} %param.15), channel_id=1, source_target_pairs={{0,16},{1,17},{2,18},{3,19},{4,20},{5,21},{6,22},{7,23},{8,24},{9,... | collective-permute-start | bytes 25165832 | tf_op jit(solution)/shard_map/ppermute | solution.py:40
  3.2 22.8 %collective-permute-start.7 = (bf16[4096,256]{1,0:T(8,128)(2,1)}, bf16[4096,256]{1,0:T(8,128)(2,1)S(1)}, u32[]{:S(2)}, u32[]{:S(2)}) collective-permute-start(bf16[4096,256]{1,0:T(8,128)(2,1)} %param.18), channel_id=1, source_target_pairs={{0,16},{1,17},{2,18},{3,19},{4,20},{5,21},{6,22},{7,23},{8,24},{9,... | collective-permute-start | bytes 6291464 | tf_op jit(solution)/shard_map/ppermute | solution.py:40
  8.0 7.3 %collective-permute-start.2 = (bf16[2,32,384]{2,1,0:T(8,128)(2,1)S(1)}, bf16[2,32,384]{2,1,0:T(8,128)(2,1)S(1)}, u32[]{:S(2)}, u32[]{:S(2)}) collective-permute-start(bf16[2,32,384]{2,1,0:T(8,128)(2,1)S(1)} %pad_maximum_fusion.5), channel_id=1, source_target_pairs={{0,129},{1,128},{2,131},{3,130},{4,133},{5,132},{6,135},{7,134},{8... | collective-permute-start | bytes 147464 | tf_op jit(solution)/shard_map/ppermute | solution.py:40
  9.7 7.7 %collective-permute-start.3 = (bf16[2,32,896]{2,1,0:T(8,128)(2,1)S(1)}, bf16[2,32,896]{2,1,0:T(8,128)(2,1)S(1)}, u32[]{:S(2)}, u32[]{:S(2)}) collective-permute-start(bf16[2,32,896]{2,1,0:T(8,128)(2,1)S(1)} %pad_maximum_fusion.3), channel_id=1, source_target_pairs={{0,14},{1,15},{2,4},{3,5},{4,2},{5,3},{6,8},{7,9},{8,6},{9,7},{10,... | collective-permute-start | bytes 344072 | tf_op jit(solution)/shard_map/ppermute | solution.py:40
  19.0 6.9 %collective-permute-start.6 = (bf16[2,32,896]{2,1,0:T(8,128)(2,1)S(1)}, bf16[2,32,896]{2,1,0:T(8,128)(2,1)S(1)}, u32[]{:S(2)}, u32[]{:S(2)}) collective-permute-start(bf16[2,32,896]{2,1,0:T(8,128)(2,1)S(1)} %collective-permute-done.3), channel_id=1, source_target_pairs={{0,4},{1,5},{2,14},{3,15},{4,8},{5,9},{6,2},{7,3},{8,12},{9,13},{1... | collective-permute-start | bytes 344072 | tf_op jit(solution)/shard_map/ppermute | solution.py:40
  26.1 10.0 %collective-permute-start.9 = (bf16[1,8,32,896]{3,2,1,0:T(8,128)(2,1)S(1)}, bf16[1,8,32,896]{3,2,1,0:T(8,128)(2,1)}, u32[]{:S(2)}, u32[]{:S(2)}) collective-permute-start(bf16[1,8,32,896]{3,2,1,0:T(8,128)(2,1)S(1)} %bitcast.28), channel_id=1, source_target_pairs={{0,32},{1,33},{2,34},{3,35},{4,36},{5,37},{6,38},{7,39},{8,40},{9,... | collective-permute-start | bytes 1376264 | tf_op jit(solution)/shard_map/ppermute | solution.py:40
  26.4 11.8 %collective-permute-start.10 = (bf16[1,8,32,896]{3,2,1,0:T(8,128)(2,1)S(1)}, bf16[1,8,32,896]{3,2,1,0:T(8,128)(2,1)S(1)}, u32[]{:S(2)}, u32[]{:S(2)}) collective-permute-start(bf16[1,8,32,896]{3,2,1,0:T(8,128)(2,1)S(1)} %bitcast.29), channel_id=1, source_target_pairs={{0,96},{1,97},{2,98},{3,99},{4,100},{5,101},{6,102},{7,103},{8,104... | collective-permute-start | bytes 1376264 | tf_op jit(solution)/shard_map/ppermute | solution.py:40
  29.9 8.3 %collective-permute-start.11 = (bf16[8,32,384]{2,1,0:T(8,128)(2,1)S(1)}, bf16[8,32,384]{2,1,0:T(8,128)(2,1)S(1)}, u32[]{:S(2)}, u32[]{:S(2)}) collective-permute-start(bf16[8,32,384]{2,1,0:T(8,128)(2,1)S(1)} %pad_maximum_fusion.2), channel_id=1, source_target_pairs={{0,96},{1,97},{2,98},{3,99},{4,100},{5,101},{6,102},{7,103},{8,104... | collective-permute-start | bytes 589832 | tf_op jit(solution)/shard_map/ppermute | solution.py:40
  38.2 17.4 %collective-permute-start.13 = (bf16[2,8,32,896]{3,2,1,0:T(8,128)(2,1)S(1)}, bf16[2,8,32,896]{3,2,1,0:T(8,128)(2,1)}, u32[]{:S(2)}, u32[]{:S(2)}) collective-permute-start(bf16[2,8,32,896]{3,2,1,0:T(8,128)(2,1)S(1)} %pad_maximum_fusion.refs_3_), channel_id=1, source_target_pairs={{0,128},{1,129},{2,130},{3,131},{4,132},{5,133},{6,134},{7,135},{8... | collective-permute-start | bytes 2752520 | tf_op jit(solution)/shard_map/ppermute | solution.py:40
  38.2 17.4 %collective-permute-start.14 = (bf16[2,8,32,896]{3,2,1,0:T(8,128)(2,1)S(1)}, bf16[2,8,32,896]{3,2,1,0:T(8,128)(2,1)}, u32[]{:S(2)}, u32[]{:S(2)}) collective-permute-start(bf16[2,8,32,896]{3,2,1,0:T(8,128)(2,1)S(1)} %pad_maximum_fusion.refs_3_), channel_id=1, source_target_pairs={{0,129},{1,128},{2,131},{3,130},{4,133},{5,132},{6,135},{7,134},{8... | collective-permute-start | bytes 2752520 | tf_op jit(solution)/shard_map/ppermute | solution.py:40
  40.8 12.9 %collective-permute-start.12 = (bf16[1,8,32,896]{3,2,1,0:T(8,128)(2,1)}, bf16[1,8,32,896]{3,2,1,0:T(8,128)(2,1)}, u32[]{:S(2)}, u32[]{:S(2)}) collective-permute-start(bf16[1,8,32,896]{3,2,1,0:T(8,128)(2,1)} %collective-permute-done.9), channel_id=1, source_target_pairs={{0,32},{1,33},{2,34},{3,35},{4,36},{5,37},{6,38},{7,39},{8,40},{9,... | collective-permute-start | bytes 1376264 | tf_op jit(solution)/shard_map/ppermute | solution.py:40
  43.2 12.4 %collective-permute-start.15 = (bf16[16,32,384]{2,1,0:T(8,128)(2,1)S(1)}, bf16[16,32,384]{2,1,0:T(8,128)(2,1)}, u32[]{:S(2)}, u32[]{:S(2)}) collective-permute-start(bf16[16,32,384]{2,1,0:T(8,128)(2,1)S(1)} %constant_dynamic-update-slice_fusion.2.refs_11_), channel_id=1, source_target_pairs={{0,2},{1,3},{2,4},{3,5},{4,6},{5,7},{6,8},{7,9},{8,10},{9,11},{10,... | collective-permute-start | bytes 1179656 | tf_op jit(solution)/shard_map/ppermute | solution.py:40
  43.3 12.3 %collective-permute-start.16 = (bf16[16,32,384]{2,1,0:T(8,128)(2,1)S(1)}, bf16[16,32,384]{2,1,0:T(8,128)(2,1)}, u32[]{:S(2)}, u32[]{:S(2)}) collective-permute-start(bf16[16,32,384]{2,1,0:T(8,128)(2,1)S(1)} %constant_dynamic-update-slice_fusion.2.refs_11_), channel_id=1, source_target_pairs={{0,14},{1,15},{2,0},{3,1},{4,2},{5,3},{6,4},{7,5},{8,6},{9,7},{10,... | collective-permute-start | bytes 1179656 | tf_op jit(solution)/shard_map/ppermute | solution.py:40
  55.6 14.3 %collective-permute-start.17 = (bf16[2,8,32,896]{3,2,1,0:T(8,128)(2,1)}, bf16[2,8,32,896]{3,2,1,0:T(8,128)(2,1)}, u32[]{:S(2)}, u32[]{:S(2)}) collective-permute-start(bf16[2,8,32,896]{3,2,1,0:T(8,128)(2,1)} %constant_dynamic-update-slice_fusion.refs_4_), channel_id=1, source_target_pairs={{0,128},{1,129},{2,130},{3,131},{4,132},{5,133},{6,134},{7,135},{8... | collective-permute-start | bytes 2752520 | tf_op jit(solution)/shard_map/ppermute | solution.py:40
  55.9 14.1 %collective-permute-start.18 = (bf16[2,8,32,896]{3,2,1,0:T(8,128)(2,1)}, bf16[2,8,32,896]{3,2,1,0:T(8,128)(2,1)}, u32[]{:S(2)}, u32[]{:S(2)}) collective-permute-start(bf16[2,8,32,896]{3,2,1,0:T(8,128)(2,1)} %constant_dynamic-update-slice_fusion.refs_4_), channel_id=1, source_target_pairs={{0,129},{1,128},{2,131},{3,130},{4,133},{5,132},{6,135},{7,134},{8... | collective-permute-start | bytes 2752520 | tf_op jit(solution)/shard_map/ppermute | solution.py:40
  58.6 8.4 %collective-permute-start.21 = (bf16[16,32,384]{2,1,0:T(8,128)(2,1)}, bf16[16,32,384]{2,1,0:T(8,128)(2,1)}, u32[]{:S(2)}, u32[]{:S(2)}) collective-permute-start(bf16[16,32,384]{2,1,0:T(8,128)(2,1)} %collective-permute-done.15.refs_12_), channel_id=1, source_target_pairs={{0,2},{1,3},{2,4},{3,5},{4,6},{5,7},{6,8},{7,9},{8,10},{9,11},{10,... | collective-permute-start | bytes 1179656 | tf_op jit(solution)/shard_map/ppermute | solution.py:40
  58.6 8.5 %collective-permute-start.22 = (bf16[16,32,384]{2,1,0:T(8,128)(2,1)}, bf16[16,32,384]{2,1,0:T(8,128)(2,1)}, u32[]{:S(2)}, u32[]{:S(2)}) collective-permute-start(bf16[16,32,384]{2,1,0:T(8,128)(2,1)} %collective-permute-done.16.refs_13_), channel_id=1, source_target_pairs={{0,14},{1,15},{2,0},{3,1},{4,2},{5,3},{6,4},{7,5},{8,6},{9,7},{10,... | collective-permute-start | bytes 1179656 | tf_op jit(solution)/shard_map/ppermute | solution.py:40
  67.1 9.3 %collective-permute-start.23 = (bf16[16,32,384]{2,1,0:T(8,128)(2,1)}, bf16[16,32,384]{2,1,0:T(8,128)(2,1)S(1)}, u32[]{:S(2)}, u32[]{:S(2)}) collective-permute-start(bf16[16,32,384]{2,1,0:T(8,128)(2,1)} %collective-permute-done.21.refs_14_), channel_id=1, source_target_pairs={{0,2},{1,3},{2,4},{3,5},{4,6},{5,7},{6,8},{7,9},{8,10},{9,11},{10,... | collective-permute-start | bytes 1179656 | tf_op jit(solution)/shard_map/ppermute | solution.py:40
  67.1 9.3 %collective-permute-start.24 = (bf16[16,32,384]{2,1,0:T(8,128)(2,1)}, bf16[16,32,384]{2,1,0:T(8,128)(2,1)S(1)}, u32[]{:S(2)}, u32[]{:S(2)}) collective-permute-start(bf16[16,32,384]{2,1,0:T(8,128)(2,1)} %collective-permute-done.22.refs_15_), channel_id=1, source_target_pairs={{0,14},{1,15},{2,0},{3,1},{4,2},{5,3},{6,4},{7,5},{8,6},{9,7},{10,... | collective-permute-start | bytes 1179656 | tf_op jit(solution)/shard_map/ppermute | solution.py:40
  69.9 17.7 %collective-permute-start.20 = (bf16[2,8,32,896]{3,2,1,0:T(8,128)(2,1)}, bf16[2,8,32,896]{3,2,1,0:T(8,128)(2,1)}, u32[]{:S(2)}, u32[]{:S(2)}) collective-permute-start(bf16[2,8,32,896]{3,2,1,0:T(8,128)(2,1)} %collective-permute-done.18.refs_8_), channel_id=1, source_target_pairs={{0,129},{1,128},{2,131},{3,130},{4,133},{5,132},{6,135},{7,134},{8... | collective-permute-start | bytes 2752520 | tf_op jit(solution)/shard_map/ppermute | solution.py:40
  72.6 15.0 %collective-permute-start.19 = (bf16[2,8,32,896]{3,2,1,0:T(8,128)(2,1)}, bf16[2,8,32,896]{3,2,1,0:T(8,128)(2,1)}, u32[]{:S(2)}, u32[]{:S(2)}) collective-permute-start(bf16[2,8,32,896]{3,2,1,0:T(8,128)(2,1)} %collective-permute-done.13.refs_5_), channel_id=1, source_target_pairs={{0,128},{1,129},{2,130},{3,131},{4,132},{5,133},{6,134},{7,135},{8... | collective-permute-start | bytes 2752520 | tf_op jit(solution)/shard_map/ppermute | solution.py:40
  77.9 9.6 %collective-permute-start.25 = (bf16[16,32,384]{2,1,0:T(8,128)(2,1)}, bf16[16,32,384]{2,1,0:T(8,128)(2,1)}, u32[]{:S(2)}, u32[]{:S(2)}) collective-permute-start(bf16[16,32,384]{2,1,0:T(8,128)(2,1)} %broadcast_select_fusion), channel_id=1, source_target_pairs={{0,2},{1,3},{2,4},{3,5},{4,6},{5,7},{6,8},{7,9},{8,10},{9,11},{10,... | collective-permute-start | bytes 1179656 | tf_op jit(solution)/shard_map/ppermute | solution.py:40
  119.8 18.1 %collective-permute-start.31 = (f32[8,256]{1,0:T(8,128)S(1)}, f32[8,256]{1,0:T(8,128)S(1)}, u32[]{:S(2)}, u32[]{:S(2)}) collective-permute-start(f32[8,256]{1,0:T(8,128)S(1)} %maximum_maximum_fusion.4), channel_id=1, source_target_pairs={{0,14},{1,15},{2,4},{3,5},{4,2},{5,3},{6,8},{7,9},{8,6},{9,7},{10,... | collective-permute-start | bytes 24584 | tf_op jit(solution)/shard_map/ppermute | solution.py:40
  123.0 24.3 %collective-permute-start.34 = (f32[2,256,256]{2,1,0:T(8,128)S(1)}, f32[2,256,256]{2,1,0:T(8,128)S(1)}, u32[]{:S(2)}, u32[]{:S(2)}) collective-permute-start(f32[2,256,256]{2,1,0:T(8,128)S(1)} %get-tuple-element.36), channel_id=1, source_target_pairs={{0,16},{1,17},{2,18},{3,19},{4,20},{5,21},{6,22},{7,23},{8,24},{9,... | collective-permute-start | bytes 1572872 | tf_op jit(solution)/shard_map/ppermute | solution.py:40
  (18 other events, 87.7 us)
